TPU v7x, 32 devices: a whole 2x2x4 slice. The times are simulated.
32 devices in a mesh: dp: 8 (over y, x, core), tensor: 4 (over z).
Axes of the slice: x: 2, y: 2, z: 4, core: 2. Of those that a mesh axis runs over, the one named last changes fastest.
Arguments:
- hidden_in: float32 [6144, 2048], P('dp', 'tensor'), may hold values from -30 to 30
- gain: float32 [2048], replicated, may hold values from 0.5 to 1.5
- bias: float32 [2048], replicated, may hold values from -1 to 1
- w_qkv: bfloat16 [2048, 3, 2048], P(None, None, 'tensor'), may hold values from -0.125 to 0.125
- b_qkv: float32 [3, 2048], P(None, 'tensor'), may hold values from -1 to 1
- w_dense: bfloat16 [2048, 2048], P('tensor'), may hold values from -1.5 to 1.5
- b_dense: float32 [2048], P('tensor'), may hold values from -1 to 1
- w_fc1: bfloat16 [2048, 8192], P(None, 'tensor'), may hold values from -1 to 1
- b_fc1: float32 [8192], P('tensor'), may hold values from -1 to 1
- w_fc2: bfloat16 [8192, 2048], P('tensor'), may hold values from -0.0625 to 0.0625
- b_fc2: float32 [2048], P('tensor'), may hold values from -1 to 1
- cotangent: float32 [6144, 2048], P('dp', 'tensor'), may hold values from -6 to 6
- seq_lengths: int32 [3], replicated, may hold values from 1 to 32, 48 in all
- padding: int32 [3], replicated, may hold values from 0 to 127
- block_perm: int32 [48], replicated, may hold values from 0 to 47, each once
Outputs:
- output: float32 [6144, 2048], P('dp', 'tensor')
- grad_input: float32 [6144, 2048], P('dp', 'tensor')
- grad_gain: float32 [2048], P('tensor')
- grad_bias: float32 [2048], P('tensor')
- grad_w_qkv: float32 [2048, 3, 2048], P(None, None, 'tensor')
- grad_b_qkv: float32 [3, 2048], P(None, 'tensor')
- grad_w_dense: float32 [2048, 2048], P('tensor')
- grad_b_dense: float32 [2048], P('tensor')
- grad_w_fc1: float32 [2048, 8192], P(None, 'tensor')
- grad_b_fc1: float32 [8192], P('tensor')
- grad_w_fc2: float32 [8192, 2048], P('tensor')
- grad_b_fc2: float32 [2048], P('tensor')
- rms_output: float32 [], replicated
- rms_branch: float32 [], replicated
Inputs may be any that keep to these rules, and one draw needn't show every extreme that they name: `seq_lengths`: the lengths sum to 48; the longest is exactly 32. `block_perm`: each block number appears once.
All inputs are finite; a program needn't handle non-finite values.
Results may differ from a plain program's by a relative error of at most 0.025.
Values may be sent and summed in bfloat16 or wider, within the bound.
No kernel may reach another device: no remote copies, remote signals or barrier semaphores. Data moves between devices by JAX's collectives and lax.ppermute only.
A program may use at most 256 MiB of HBM per device.

v0:
```python
import jax
import jax.numpy as jnp
from jax import lax
from jax.sharding import PartitionSpec as P

HD = 64
ROT = 32
BLK = 128


epsilon = 1e-05
masked_score = -1e30


def token_table(seq_lengths, padding, initial):
    seq_count = seq_lengths.shape[0]
    seq_ends = jnp.cumsum(seq_lengths)
    seq_starts = seq_ends - seq_lengths
    seq_block = jnp.sum((initial[:, None] >= seq_ends[None, :]).astype(jnp.int32), axis=1)
    members = (seq_block[:, None] == jnp.arange(seq_count, dtype=jnp.int32)[None, :]).astype(
        jnp.int32
    )
    first_block = jnp.sum(members * seq_starts[None, :], axis=1)
    limits = jnp.sum(members * (seq_lengths * BLK - padding)[None, :], axis=1)
    offsets = jnp.arange(BLK, dtype=jnp.int32)
    positions = (initial - first_block)[:, None] * BLK + offsets[None, :]
    seq_ids = jnp.broadcast_to(seq_block[:, None], positions.shape)
    is_valid = positions < limits[:, None]
    return (seq_ids.reshape(-1), positions.reshape(-1), is_valid.reshape(-1))


def rotary_tables(positions):
    frequency = 10000.0 ** (-jnp.arange(0, ROT, 2, dtype=jnp.float32) / ROT)
    angles = positions.astype(jnp.float32)[:, None] * frequency[None, :]
    return (jnp.cos(angles)[:, None, :], jnp.sin(angles)[:, None, :])


def rotate(heads_array, cosine_table, sine_table):
    half_rot = ROT // 2
    lower_half = heads_array[..., :half_rot]
    upper_half = heads_array[..., half_rot:ROT]
    return jnp.concatenate(
        [
            lower_half * cosine_table - upper_half * sine_table,
            upper_half * cosine_table + lower_half * sine_table,
            heads_array[..., ROT:],
        ],
        axis=-1,
    )


def unrotate(heads_array, cosine_table, sine_table):
    half_rot = ROT // 2
    lower_half = heads_array[..., :half_rot]
    upper_half = heads_array[..., half_rot:ROT]
    return jnp.concatenate(
        [
            lower_half * cosine_table + upper_half * sine_table,
            upper_half * cosine_table - lower_half * sine_table,
            heads_array[..., ROT:],
        ],
        axis=-1,
    )


def gelu_tanh(gelu_input):
    return jax.nn.gelu(gelu_input, approximate=True)


def local(
    hidden_in,
    gain,
    bias,
    w_qkv,
    b_qkv,
    w_dense,
    b_dense,
    w_fc1,
    b_fc1,
    w_fc2,
    b_fc2,
    cotangent,
    seq_lengths,
    padding,
    block_perm,
):
    tok_local, dim_local = hidden_in.shape
    model_width = gain.shape[0]
    heads_local = w_qkv.shape[2] // HD
    head_width = heads_local * HD
    data_index = lax.axis_index("dp")
    tensor_index = lax.axis_index("tensor")
    score_scale = HD ** (-0.5)
    seq_all, pos_all, valid_all = token_table(seq_lengths, padding, block_perm)
    my_seq = lax.dynamic_slice_in_dim(seq_all, data_index * tok_local, tok_local)
    my_pos = lax.dynamic_slice_in_dim(pos_all, data_index * tok_local, tok_local)
    my_valid = lax.dynamic_slice_in_dim(valid_all, data_index * tok_local, tok_local)
    cosine_table, sine_table = rotary_tables(my_pos)
    full_in = lax.all_gather(hidden_in.astype(jnp.bfloat16), "tensor", axis=1, tiled=True).astype(
        hidden_in.dtype
    )
    row_mean = jnp.mean(full_in, axis=-1, keepdims=True)
    centered = full_in - row_mean
    inv_std = lax.rsqrt(jnp.mean(centered * centered, axis=-1, keepdims=True) + epsilon)
    normal_x = centered * inv_std
    normed = (normal_x * gain + bias).astype(jnp.bfloat16)
    projections = (
        jnp.einsum("td,dcf->tcf", normed, w_qkv, preferred_element_type=jnp.float32) + b_qkv
    )
    shaped = projections.reshape(tok_local, 3, heads_local, HD)
    queries = rotate(shaped[:, 0], cosine_table, sine_table).astype(jnp.bfloat16)
    keys_rot = (
        rotate(shaped[:, 1], cosine_table, sine_table)
        .astype(jnp.bfloat16)
        .reshape(tok_local, head_width)
    )
    values = shaped[:, 2].astype(jnp.bfloat16).reshape(tok_local, head_width)

    def piece_scores(key_piece, row_start):
        row_count = key_piece.shape[0]
        key_seq = lax.dynamic_slice_in_dim(seq_all, row_start, row_count)
        key_pos = lax.dynamic_slice_in_dim(pos_all, row_start, row_count)
        scores = (
            jnp.einsum(
                "qhd,khd->hqk",
                queries,
                key_piece.reshape(row_count, heads_local, HD),
                preferred_element_type=jnp.float32,
            )
            * score_scale
        )
        allowed = (key_seq[None, :] == my_seq[:, None]) & (key_pos[None, :] <= my_pos[:, None])
        return jnp.where(allowed[None], scores, masked_score)

    def forward_step(carried, pieces, row_start):
        run_max, run_sum, accumulated = carried
        key_piece, value_piece = pieces
        row_count = key_piece.shape[0]
        scores = piece_scores(key_piece, row_start)
        new_max = jnp.maximum(run_max, jnp.max(scores, axis=-1))
        factor = jnp.exp(run_max - new_max)
        weights = jnp.exp(scores - new_max[..., None])
        run_sum = run_sum * factor + jnp.sum(weights, axis=-1)
        accumulated = accumulated * factor[..., None] + jnp.einsum(
            "hqk,khd->hqd",
            weights.astype(jnp.bfloat16),
            value_piece.reshape(row_count, heads_local, HD),
            preferred_element_type=jnp.float32,
        )
        return (new_max, run_sum, accumulated)

    start_state = (
        jnp.full((heads_local, tok_local), masked_score, jnp.float32),
        jnp.zeros((heads_local, tok_local), jnp.float32),
        jnp.zeros((heads_local, tok_local, HD), jnp.float32),
    )
    key_all, value_all = (
        lax.all_gather(keys_rot, "dp", axis=0, tiled=True),
        lax.all_gather(values, "dp", axis=0, tiled=True),
    )

    def scan_forward(carried, piece_index):
        row_start = piece_index * tok_local
        pieces = (
            lax.dynamic_slice_in_dim(key_all, row_start, tok_local, 0),
            lax.dynamic_slice_in_dim(value_all, row_start, tok_local, 0),
        )
        return (forward_step(carried, pieces, row_start), None)

    folded, unused = lax.scan(
        scan_forward, start_state, jnp.arange(key_all.shape[0] // tok_local, dtype=jnp.int32)
    )
    run_max, run_sum, accumulated = folded
    log_total = run_max + jnp.log(run_sum)
    attended = jnp.transpose(accumulated / run_sum[..., None], (1, 0, 2)).reshape(
        tok_local, head_width
    )
    attended = attended.astype(jnp.bfloat16)
    hidden_pre = jnp.dot(normed, w_fc1, preferred_element_type=jnp.float32) + b_fc1
    activated = gelu_tanh(hidden_pre).astype(jnp.bfloat16)
    partial_value = jnp.dot(attended, w_dense, preferred_element_type=jnp.float32) + jnp.dot(
        activated, w_fc2, preferred_element_type=jnp.float32
    )
    projected = lax.psum_scatter(
        partial_value.astype(jnp.bfloat16), "tensor", scatter_dimension=1, tiled=True
    ).astype(jnp.float32)
    branch = projected + b_dense + b_fc2
    output = hidden_in + branch
    valid_rows = my_valid.astype(jnp.float32)[:, None]
    totals = lax.psum(
        (jnp.sum(output * output * valid_rows), jnp.sum(branch * branch * valid_rows)),
        ("dp", "tensor"),
    )
    valid_count = jnp.sum(valid_all.astype(jnp.float32)) * model_width
    rms_output = jnp.sqrt(totals[0] / valid_count)
    rms_branch = jnp.sqrt(totals[1] / valid_count)
    bias_grad = jnp.sum(cotangent, axis=0)
    grad_proj = lax.all_gather(cotangent.astype(jnp.bfloat16), "tensor", axis=1, tiled=True)
    grad_act = jnp.einsum("td,fd->tf", grad_proj, w_fc2, preferred_element_type=jnp.float32)
    grad_w_fc2 = jnp.einsum("tf,td->fd", activated, grad_proj, preferred_element_type=jnp.float32)
    unused_value, gelu_back = jax.vjp(gelu_tanh, hidden_pre)
    grad_hidden = gelu_back(grad_act)[0].astype(jnp.bfloat16)
    grad_b_fc1 = jnp.sum(grad_hidden.astype(jnp.float32), axis=0)
    grad_w_fc1 = jnp.einsum("td,tf->df", normed, grad_hidden, preferred_element_type=jnp.float32)
    grad_normed = jnp.einsum("tf,df->td", grad_hidden, w_fc1, preferred_element_type=jnp.float32)
    grad_w_dense = jnp.einsum("te,td->ed", attended, grad_proj, preferred_element_type=jnp.float32)
    grad_attended = jnp.einsum(
        "td,ed->te", grad_proj, w_dense, preferred_element_type=jnp.float32
    ).astype(jnp.bfloat16)
    grad_heads = grad_attended.reshape(tok_local, heads_local, HD)
    row_dot = jnp.transpose(
        jnp.sum(
            grad_heads.astype(jnp.float32)
            * attended.reshape(tok_local, heads_local, HD).astype(jnp.float32),
            axis=-1,
        )
    )
    piece_count = key_all.shape[0] // tok_local

    def backward_step(grad_sum, piece_index):
        row_start = piece_index * tok_local
        key_piece = lax.dynamic_slice_in_dim(key_all, row_start, tok_local, 0)
        value_piece = lax.dynamic_slice_in_dim(value_all, row_start, tok_local, 0)
        key_heads = key_piece.reshape(tok_local, heads_local, HD)
        scores = piece_scores(key_piece, row_start)
        probabilities = jnp.exp(scores - log_total[..., None])
        grad_probs = jnp.einsum(
            "qhd,khd->hqk",
            grad_heads,
            value_piece.reshape(tok_local, heads_local, HD),
            preferred_element_type=jnp.float32,
        )
        grad_scores = (probabilities * (grad_probs - row_dot[..., None])).astype(jnp.bfloat16)
        grad_sum = grad_sum + jnp.einsum(
            "hqk,khd->qhd", grad_scores, key_heads, preferred_element_type=jnp.float32
        )
        key_term = (
            jnp.einsum("hqk,qhd->khd", grad_scores, queries, preferred_element_type=jnp.float32)
            * score_scale
        )
        value_term = jnp.einsum(
            "hqk,qhd->khd",
            probabilities.astype(jnp.bfloat16),
            grad_heads,
            preferred_element_type=jnp.float32,
        )
        return (
            grad_sum,
            jnp.stack(
                [
                    key_term.reshape(tok_local, head_width),
                    value_term.reshape(tok_local, head_width),
                ],
                axis=1,
            ),
        )

    grad_sum, key_terms = lax.scan(
        backward_step,
        jnp.zeros((tok_local, heads_local, HD), jnp.float32),
        jnp.arange(piece_count, dtype=jnp.int32),
    )
    key_terms = key_terms.reshape(piece_count * tok_local, 2, head_width)
    own_terms = lax.psum_scatter(
        key_terms.astype(jnp.bfloat16), "dp", scatter_dimension=0, tiled=True
    ).astype(jnp.float32)
    key_grad_local = own_terms[:, 0].reshape(tok_local, heads_local, HD)
    value_grad_local = own_terms[:, 1]
    grad_queries = unrotate(grad_sum * score_scale, cosine_table, sine_table).reshape(
        tok_local, head_width
    )
    grad_keys = unrotate(key_grad_local, cosine_table, sine_table).reshape(tok_local, head_width)
    grad_qkv = jnp.stack([grad_queries, grad_keys, value_grad_local], axis=1).astype(jnp.bfloat16)
    grad_w_qkv = jnp.einsum("td,tcf->dcf", normed, grad_qkv, preferred_element_type=jnp.float32)
    grad_b_qkv = jnp.sum(grad_qkv.astype(jnp.float32), axis=0)
    grad_normed = grad_normed + jnp.einsum(
        "tcf,dcf->td", grad_qkv, w_qkv, preferred_element_type=jnp.float32
    )
    gain_local = lax.dynamic_slice_in_dim(gain, tensor_index * dim_local, dim_local)
    normal_local = lax.dynamic_slice_in_dim(normal_x, tensor_index * dim_local, dim_local, 1)
    grad_full = lax.psum(grad_normed.astype(jnp.bfloat16), "tensor").astype(jnp.float32)
    grad_local = lax.dynamic_slice_in_dim(grad_full, tensor_index * dim_local, dim_local, 1)
    scaled_full = grad_full * gain
    mean_one = jnp.mean(scaled_full, axis=-1, keepdims=True)
    mean_two = jnp.mean(scaled_full * normal_x, axis=-1, keepdims=True)
    scaled_local = grad_local * gain_local
    grad_input = cotangent + inv_std * (scaled_local - mean_one - normal_local * mean_two)
    gain_part = jnp.sum(grad_local * normal_local, axis=0)
    bias_part = jnp.sum(grad_local, axis=0)
    summed = (
        lax.psum(grad_w_qkv.astype(jnp.bfloat16), "dp").astype(jnp.float32),
        lax.psum(grad_b_qkv.astype(jnp.bfloat16), "dp").astype(jnp.float32),
        lax.psum(grad_w_dense.astype(jnp.bfloat16), "dp").astype(jnp.float32),
        lax.psum(grad_w_fc1.astype(jnp.bfloat16), "dp").astype(jnp.float32),
        lax.psum(grad_b_fc1.astype(jnp.bfloat16), "dp").astype(jnp.float32),
        lax.psum(grad_w_fc2.astype(jnp.bfloat16), "dp").astype(jnp.float32),
        lax.psum(gain_part.astype(jnp.bfloat16), "dp").astype(jnp.float32),
        lax.psum(bias_part.astype(jnp.bfloat16), "dp").astype(jnp.float32),
        lax.psum(bias_grad.astype(jnp.bfloat16), "dp").astype(jnp.float32),
    )
    return (
        output,
        grad_input,
        summed[6],
        summed[7],
        summed[0],
        summed[1],
        summed[2],
        summed[8],
        summed[3],
        summed[4],
        summed[5],
        summed[8],
        rms_output,
        rms_branch,
    )


def solution(mesh):
    return jax.shard_map(
        local,
        mesh=mesh,
        in_specs=(
            P("dp", "tensor"),
            P(),
            P(),
            P(None, None, "tensor"),
            P(None, "tensor"),
            P("tensor", None),
            P("tensor"),
            P(None, "tensor"),
            P("tensor"),
            P("tensor", None),
            P("tensor"),
            P("dp", "tensor"),
            P(),
            P(),
            P(),
        ),
        out_specs=(
            P("dp", "tensor"),
            P("dp", "tensor"),
            P("tensor"),
            P("tensor"),
            P(None, None, "tensor"),
            P(None, "tensor"),
            P("tensor", None),
            P("tensor"),
            P(None, "tensor"),
            P("tensor"),
            P("tensor", None),
            P("tensor"),
            P(),
            P(),
        ),
        check_vma=False,
    )
```

profile of v0, /device:TPU:0, one launch (start us, length us, event | category | flops | bytes accessed | tf_op | source)
XLA Modules:
  0.0 1502.2 jit_solution(6100520344572101025)
XLA Ops:
  15.3 61.1 %all-gather.5.cloned.1.call-done = bf16[768,2048]{1,0:T(8,128)(2,1)} async-done(((bf16[768,512]{1,0:T(8,128)(2,1)}), bf16[768,2048]{1,0:T(8,128)(2,1)}) %all-gather.5.cloned.1.call-update) | async-done | bytes 3145744 | tf_op jit(solution)/shard_map/all_gather | solution.py:99
  103.4 35.3 %all-gather.7.cloned.1.call-done = bf16[6144,512]{0,1:T(8,128)(2,1)} async-done(((bf16[768,512]{0,1:T(8,128)(2,1)}), bf16[6144,512]{0,1:T(8,128)(2,1)}) %all-gather.7.cloned.1.call-update) | async-done | bytes 6291472 | tf_op jit(solution)/shard_map/all_gather | solution.py:158
  138.7 47.8 %all-gather.9.cloned.1.call-done = bf16[6144,512]{0,1:T(8,128)(2,1)} async-done(((bf16[768,512]{0,1:T(8,128)(2,1)}), bf16[6144,512]{0,1:T(8,128)(2,1)}) %all-gather.9.cloned.1.call-update) | async-done | bytes 6291472 | tf_op jit(solution)/shard_map/all_gather | solution.py:159
  186.5 290.7 %while.28 = (s32[]{:T(128)}, f32[8,768]{1,0:T(8,128)S(1)}, f32[8,768]{1,0:T(8,128)}, f32[8,768,64]{1,2,0:T(8,128)}, s32[8]{0:T(128)S(1)}, /*index=5*/s32[6144]{0...) while((s32[]{:T(128)}, f32[8,768]{1,0:T(8,128)S(1)}, ...), condition=%wide.region_8.9_spmd.clone, body=%wide.region_5.0_spmd.clone.sunk | while | flops 1262843904 | bytes 68051488 | solution.py:170
  191.3 9.6 fusion.105
  200.9 10.3 fusion.106
  211.8 10.3 fusion.108
  227.0 9.4 fusion.105
  236.4 10.2 fusion.106
  247.9 10.7 fusion.108
  272.8 10.2 fusion.106
  284.4 10.7 fusion.108
  309.2 10.2 fusion.106
  320.8 10.7 fusion.108
  345.7 10.2 fusion.106
  357.2 10.7 fusion.108
  382.1 10.2 fusion.106
  393.7 10.7 fusion.108
  418.5 10.2 fusion.106
  430.1 10.7 fusion.108
  454.9 10.2 fusion.106
  466.5 10.7 fusion.108
  483.4 365.2 %while.29 = (s32[]{:T(128)}, f32[768,8,64]{0,2,1:T(8,128)}, bf16[8,768,2,512]{1,3,2,0:T(8,128)(2,1)}, s32[8]{0:T(128)S(1)}, bf16[6144,512]{0,1:T(8,128)(2,1)}, /...) while((s32[]{:T(128)}, f32[768,8,64]{0,2,1:T(8,128)}, ...), condition=%wide.region_12.13_spmd.clone, body=%wide.region_11.12_spmd.clone.sunk | while | flops 3073572864 | bytes 144212784 | solution.py:258
  497.6 9.7 fusion.120
  542.9 9.8 fusion.120
  588.5 9.8 fusion.120
  634.2 9.8 fusion.120
  679.9 9.7 fusion.120
  725.6 9.7 fusion.120
  771.3 9.8 fusion.120
  816.9 9.7 fusion.120
  848.6 16.6 %copy.55 = bf16[8,768,2,512]{3,1,0,2:T(8,128)(2,1)} copy(bf16[8,768,2,512]{1,3,2,0:T(8,128)(2,1)} %get-tuple-element.155) | data formatting | bytes 25165824 | tf_op jit(solution)/shard_map/convert_element_type | solution.py:265
  866.0 10.7 fusion.44
  880.5 15.4 %fusion.46 = (bf16[2048]{0:T(1024)(128)(2,1)S(1)}, bf16[768,2048]{1,0:T(8,128)(2,1)}) fusion(f32[768,2048]{1,0:T(8,128)S(1)} %fusion.44, f32[2048]{0:T(1024)S(1)} %copy-done.39, bf16[768,2048]{1,0:T(8,128)(2,1)S(1)} %copy-done.12, bf16[2048,2048]{1,0:T(8,128)(2,1)} %param.28), kind=kOutput, calls=%fused_computation.120 | convolution fusion | flops 6477051904 | bytes 20983808 | tf_op jit(solution)/shard_map/td,fd->tf/dot_general | solution.py:199
  895.9 9.8 fusion.43
  909.8 12.3 fusion.50
  922.1 14.8 convolution_convert_fusion
  938.2 19.4 %reduce-scatter.5.cloned.1.call-done = bf16[768,2,512]{2,0,1:T(8,128)(2,1)} async-done(((bf16[6144,2,512]{2,0,1:T(8,128)(2,1)}), bf16[768,2,512]{2,0,1:T(8,128)(2,1)}) %reduce-scatter.5.cloned.1.call-update) | async-done | bytes 1572880 | tf_op jit(solution)/shard_map/reduce_scatter | solution.py:264
  968.3 9.7 fusion.32
  978.4 12.0 convolution_convert_fusion.1
  1003.4 17.4 %reduce-scatter.3.cloned.1.call-done = bf16[768,512]{1,0:T(8,128)(2,1)} async-done(((bf16[768,2048]{1,0:T(8,128)(2,1)}), bf16[768,512]{1,0:T(8,128)(2,1)}) %reduce-scatter.3.cloned.1.call-update) | async-done | bytes 786448 | tf_op jit(solution)/shard_map/reduce_scatter | solution.py:184
  1024.7 44.3 %all-reduce = (f32[]{:T(128)}, f32[]{:T(128)}) all-reduce(f32[]{:T(128)} %get-tuple-element.245, f32[]{:T(128)} %get-tuple-element.244), channel_id=1, replica_groups=mesh['dp'=8,'tensor'=4] {'dp','tensor'}, use_global_device_ids=true, to_apply=%region_33.34 | all-reduce | flops 2 | bytes 16 | tf_op jit(solution)/shard_map/psum | solution.py:190
  1072.2 72.7 %all-reduce.6.cloned.1.call-done = bf16[768,2048]{1,0:T(8,128)(2,1)} async-done(((bf16[768,2048]{1,0:T(8,128)(2,1)}), bf16[768,2048]{1,0:T(8,128)(2,1)}) %all-reduce.6.cloned.1.call-update) | async-done | bytes 3145744 | tf_op jit(solution)/shard_map/psum | solution.py:281
  1152.8 25.5 %all-reduce.1 = (bf16[512]{0:T(512)(128)(2,1)S(1)}, bf16[512]{0:T(512)(128)(2,1)S(1)}, bf16[3,512]{1,0:T(4,128)(2,1)S(1)}, bf16[512]{0:T(512)(128)(2,1)S(1)}, bf16[2048]{0:T(1024)(128)(2,1)S(1)}) all-reduce(bf16[512]{0:T(512)(128)(2,1)S(1)} %get-tuple-element.241, ...), channel_id=1, replica_groups=mesh['dp'=8,'tensor'=4] {'dp'}, use_global_device_ids=true, to_apply=%region_18.19 | all-reduce | flops 5120 | bytes 20480 | tf_op jit(solution)/shard_map/psum | solution.py:297
  1180.7 276.0 %all-reduce.8.cloned.1.call-done = (bf16[2048,3,512]{2,0,1:T(8,128)(2,1)}, bf16[512,2048]{1,0:T(8,128)(2,1)}, bf16[2048,2048]{1,0:T(8,128)(2,1)}, bf16[2048,2048]{1,0:T(8,128)(2,1)}) async-done(((bf16[2048,3,512]{2,0,1:T(8,128)(2,1)}, bf16[512,2048]{1,0:T(8,128)(2,1)}, bf16[2048,2048]{1,0:T(8,128)(2,1)}, bf16[2048,2048]{1,0:T(8,128)(2,1)}), (bf16[2048,3,512]{2,0,1:T(8,128)(2,1)}, ...) | async-done | bytes 25165840 | tf_op jit(solution)/shard_map/psum | solution.py:291
  1456.7 11.7 convert_element_type.179
  1468.4 11.7 convert_element_type.182
  1480.1 9.5 convert_element_type.172
  (383 shorter events, 474.0 us)
Async XLA Ops:
  7.2 470.8 %copy-start = (bf16[512,2048]{1,0:T(8,128)(2,1)S(1)}, bf16[512,2048]{1,0:T(8,128)(2,1)}, u32[]{:S(2)}) copy-start(bf16[512,2048]{1,0:T(8,128)(2,1)} %param.24) | copy-start | bytes 6291460
  7.2 74.6 %copy-start.29 = (f32[2048]{0:T(1024)S(1)}, f32[2048]{0:T(1024)}, u32[]{:S(2)}) copy-start(f32[2048]{0:T(1024)} %param.20) | copy-start | bytes 24580
  7.2 74.6 %copy-start.40 = (f32[2048]{0:T(1024)S(1)}, f32[2048]{0:T(1024)}, u32[]{:S(2)}) copy-start(f32[2048]{0:T(1024)} %param.21) | copy-start | bytes 24580
  7.2 74.6 %copy-start.38 = (f32[3,512]{1,0:T(4,128)S(1)}, f32[3,512]{1,0:T(4,128)}, u32[]{:S(2)}) copy-start(f32[3,512]{1,0:T(4,128)} %param.23) | copy-start | bytes 18436
  7.2 69.1 %all-gather.5.cloned.1.call-start = ((), (), s32[]{:S(2)}) async-start(), calls=%async_computation.2 | async-start | bytes 3932160 | tf_op jit(solution)/shard_map/all_gather | solution.py:99
  9.8 128.9 %all-gather.7.cloned.1.call-start = ((), (), s32[]{:S(2)}) async-start(), calls=%async_computation.3 | async-start | bytes 7077888 | tf_op jit(solution)/shard_map/all_gather | solution.py:158
  15.3 76.1 %copy-start.20 = (f32[768,16]{0,1:T(8,128)}, f32[768,16]{0,1:T(8,128)S(1)}, u32[]{:S(2)}) copy-start(f32[768,16]{0,1:T(8,128)S(1)} %get-tuple-element.345) | copy-start | bytes 147460
  15.3 76.1 %copy-start.22 = (f32[768,16]{0,1:T(8,128)}, f32[768,16]{0,1:T(8,128)S(1)}, u32[]{:S(2)}) copy-start(f32[768,16]{0,1:T(8,128)S(1)} %get-tuple-element.346) | copy-start | bytes 147460
  78.9 12.1 copy-start.24
  81.8 9.2 copy-start.26
  94.7 91.8 %all-gather.9.cloned.1.call-start = ((), (), s32[]{:S(2)}) async-start(), calls=%async_computation.4 | async-start | bytes 7077888 | tf_op jit(solution)/shard_map/all_gather | solution.py:159
  97.1 380.8 %all-gather.11.cloned.1.call-start = ((), (), s32[]{:S(2)}) async-start(), calls=%async_computation.6 | async-start | bytes 3932160 | tf_op jit(solution)/shard_map/all_gather | solution.py:198
  99.6 858.0 %reduce-scatter.5.cloned.1.call-start = ((), (), s32[]{:S(2)}) async-start(), calls=%async_computation.7 | async-start | bytes 14155776 | tf_op jit(solution)/shard_map/reduce_scatter | solution.py:264
  211.8 10.3 copy-start.43
  247.9 10.7 copy-start.43
  284.4 10.7 copy-start.43
  320.8 10.7 copy-start.43
  357.2 10.7 copy-start.43
  393.7 10.7 copy-start.43
  430.1 10.7 copy-start.43
  466.5 10.7 copy-start.43
  507.4 13.7 copy-start.1
  552.6 13.7 copy-start.1
  598.3 13.7 copy-start.1
  644.0 13.7 copy-start.1
  689.7 13.7 copy-start.1
  735.4 13.7 copy-start.1
  781.0 13.7 copy-start.1
  826.7 13.7 copy-start.1
  865.3 15.3 %copy-start.39 = (f32[2048]{0:T(1024)S(1)}, f32[2048]{0:T(1024)}, u32[]{:S(2)}) copy-start(f32[2048]{0:T(1024)} %param.27) | copy-start | bytes 24580
  865.3 155.5 %reduce-scatter.3.cloned.1.call-start = ((), (), s32[]{:S(2)}) async-start(), calls=%async_computation.5 | async-start | bytes 3932160 | tf_op jit(solution)/shard_map/reduce_scatter | solution.py:184
  866.0 14.6 copy-start.12
  866.0 30.0 %slice-start = ((s8[8388608]{0:T(1024)(128)(4,1)}), s8[4194304]{0:T(1024)(128)(4,1)S(1)}, s32[]{:S(2)}) async-start(s8[8388608]{0:T(1024)(128)(4,1)} %bitcast.189), calls=%async_computation.10 | async-start | bytes 8388608
  880.5 15.4 %slice-start.1 = ((s8[8388608]{0:T(1024)(128)(4,1)}), s8[4194304]{0:T(1024)(128)(4,1)S(1)}, s32[]{:S(2)}) async-start(s8[8388608]{0:T(1024)(128)(4,1)} %bitcast.189), calls=%async_computation.11 | async-start | bytes 8388608
  895.9 9.8 copy-start.17
  909.5 235.4 %all-reduce.6.cloned.1.call-start = ((), (), s32[]{:S(2)}) async-start(), calls=%async_computation.8 | async-start | bytes 6291456 | tf_op jit(solution)/shard_map/psum | solution.py:281
  909.7 12.3 copy-start.13
  922.1 14.8 copy-start.2
  936.8 24.9 %copy-start.21 = (f32[768,16]{0,1:T(8,128)S(1)}, f32[768,16]{0,1:T(8,128)}, u32[]{:S(2)}) copy-start(f32[768,16]{0,1:T(8,128)} %copy-done.20) | copy-start | bytes 147460
  936.8 24.9 %copy-start.23 = (f32[768,16]{0,1:T(8,128)S(1)}, f32[768,16]{0,1:T(8,128)}, u32[]{:S(2)}) copy-start(f32[768,16]{0,1:T(8,128)} %copy-done.22) | copy-start | bytes 147460
  978.1 478.6 %all-reduce.8.cloned.1.call-start = ((), (), s32[]{:S(2)}) async-start(), calls=%async_computation.9 | async-start | bytes 50331648 | tf_op jit(solution)/shard_map/psum | solution.py:291
  978.3 12.0 copy-start.14
  978.3 12.0 copy-start.18
  1001.4 19.4 %copy-start.28 = (f32[768]{0:T(1024)S(1)}, f32[768]{0:T(1024)}, u32[]{:S(2)}) copy-start(f32[768]{0:T(1024)} %get-tuple-element.314) | copy-start | bytes 9220
  1001.4 19.4 %copy-start.32 = (f32[512]{0:T(512)S(1)}, f32[512]{0:T(512)}, u32[]{:S(2)}) copy-start(f32[512]{0:T(512)} %param.29) | copy-start | bytes 6148
  1001.4 19.4 %copy-start.33 = (f32[512]{0:T(512)S(1)}, f32[512]{0:T(512)}, u32[]{:S(2)}) copy-start(f32[512]{0:T(512)} %param.25) | copy-start | bytes 6148
  1179.6 312.5 %copy-start.31 = (f32[512]{0:T(512)}, f32[512]{0:T(512)S(1)}, u32[]{:S(2)}) copy-start(f32[512]{0:T(512)S(1)} %convert_element_type.177) | copy-start | bytes 6148
  1480.1 9.5 copy-start.16
  (35 other events, 124.0 us)
Sparse Core Ops, SparseCore 0:
  10.2 66.1 all-gather.4
  94.8 43.8 all-gather.6
  141.2 45.2 all-gather.8
  188.5 63.4 all-gather.10
  865.4 92.1 reduce-scatter.4
  960.3 60.4 reduce-scatter.2
  1023.1 121.8 all-reduce.5
  1150.3 306.3 all-reduce.7
where the time goes:
time: 1510 us; the launch traced here: 1500 us
  matrix products  590 us (39%)
  waiting for transfers between devices  530 us (35%)
  other arithmetic  183 us (12%)
  local copies, waits for them, and re-layouts  98 us (6%)
  blocking collectives  69.9 us (5%)
  between operations  19.4 us (1%)
    psum x1, waiting for transfers between devices, local(): lax.psum(grad_w_qkv.astype(jnp.bfloat16), 'dp').astype(jnp.float32)  276 us
    dot_general x16, matrix products, piece_scores(): jnp.einsum('qhd,khd->hqk', queries, key_piece.reshape(row_count, heads_lo...  148 us
    dot_general x8, matrix products, forward_step(): jnp.einsum('hqk,khd->hqd', weights.astype(jnp.bfloat16), value_piece.resh...  85.1 us
    reduce_sum x8, other arithmetic, forward_step(): run_sum = run_sum * factor + jnp.sum(weights, axis=-1)  81.7 us
    dot_general x8, matrix products, backward_step(): jnp.einsum('qhd,khd->hqk', grad_heads, value_piece.reshape(tok_local, hea...  78 us
    psum x1, waiting for transfers between devices, local(): lax.psum(grad_normed.astype(jnp.bfloat16), 'tensor').astype(jnp.float32)  72.7 us
    dot_general x8, matrix products, backward_step(): jnp.einsum('hqk,qhd->khd', probabilities.astype(jnp.bfloat16), grad_heads...  72 us
    all_gather x1, waiting for transfers between devices, local(): lax.all_gather(hidden_in.astype(jnp.bfloat16), 'tensor', axis=1, tiled=True)  61.1 us
  transfers between devices with their start and end apart: 8, of which 7 were waited for; matrix products, arithmetic and copies ran while one was open for 28% of the time, Pallas kernels for 0%

commit v1 on v0

v1 whole, which is shorter than its diff:
```python
import functools

import jax
import jax.numpy as jnp
from jax import lax
from jax.experimental import pallas as pl
from jax.experimental.pallas import tpu as pltpu
from jax.sharding import PartitionSpec as P

HD = 64
ROT = 32
HALF = ROT // 2
BLK = 128
TILE = 512
LANES = 128

epsilon = 1e-05
masked_score = -1e30
far_score = 1e30
log2e = 1.4426950408889634
f32 = jnp.float32
bf16 = jnp.bfloat16


def token_table(seq_lengths, padding, initial):
    seq_count = seq_lengths.shape[0]
    seq_ends = jnp.cumsum(seq_lengths)
    seq_starts = seq_ends - seq_lengths
    seq_block = jnp.sum((initial[:, None] >= seq_ends[None, :]).astype(jnp.int32), axis=1)
    members = (seq_block[:, None] == jnp.arange(seq_count, dtype=jnp.int32)[None, :]).astype(
        jnp.int32
    )
    first_block = jnp.sum(members * seq_starts[None, :], axis=1)
    limits = jnp.sum(members * (seq_lengths * BLK - padding)[None, :], axis=1)
    offsets = jnp.arange(BLK, dtype=jnp.int32)
    positions = (initial - first_block)[:, None] * BLK + offsets[None, :]
    is_valid = positions < limits[:, None]
    return (positions.reshape(-1), is_valid.reshape(-1))


def rotary_tables(positions):
    frequency = 10000.0 ** (-jnp.arange(0, ROT, 2, dtype=f32) / ROT)
    angles = frequency[:, None] * positions.astype(f32)[None, :]
    return (jnp.cos(angles), jnp.sin(angles))


def gelu_tanh(gelu_input):
    return jax.nn.gelu(gelu_input, approximate=True)


def dot_f32(a, b):
    return lax.dot_general(a, b, (((1,), (0,)), ((), ())), preferred_element_type=f32)


def flip(block):
    return jnp.transpose(block.astype(f32)).astype(bf16)


def each_query_tile(seq_ref, rank_ref, seq_count, split, body):
    def one_seq(s, count):
        start = seq_ref[0, s] * BLK
        length = seq_ref[1, s] * BLK
        tiles = (length + TILE - 1) // TILE

        def one_tile(i, unused):
            if split == 1:
                body(start, length, i, tiles)
            else:

                @pl.when(lax.rem(count + i, split) == rank_ref[0])
                def _():
                    body(start, length, i, tiles)

            return unused

        lax.fori_loop(0, tiles, one_tile, 0)
        return count + tiles

    lax.fori_loop(0, seq_count, one_seq, 0)


def forward_kernel(seq_count, slots, subs, split, place_ref, seq_ref, rank_ref, *refs):
    parts, outs, lse_ref, seq_out_ref, q_t, keys, v_t = refs
    tokens = slots * subs * BLK
    tail = q_t.shape[1] - tokens
    q_t[:, pl.ds(tokens, tail)] = jnp.zeros((HD, tail), bf16)
    v_t[:, pl.ds(tokens, tail)] = jnp.zeros((HD, tail), bf16)
    keys[pl.ds(tokens, tail), :] = jnp.zeros((tail, HD), bf16)
    if split > 1:
        lse_ref[...] = jnp.zeros(lse_ref.shape, f32)
        seq_out_ref[...] = jnp.zeros(seq_out_ref.shape, bf16)
    for s in range(slots):
        for b in range(subs):
            where = pl.multiple_of(place_ref[s * subs + b] * BLK, BLK)
            cols = slice(b * BLK, (b + 1) * BLK)
            q_t[:, pl.ds(where, BLK)] = parts[s, 0:HD, cols]
            keys[pl.ds(where, BLK), :] = flip(parts[s, HD : 2 * HD, cols])
            v_t[:, pl.ds(where, BLK)] = parts[s, 2 * HD :, cols]
    scale = HD ** (-0.5) * log2e
    row = lax.broadcasted_iota(jnp.int32, (TILE, TILE), 0)
    col = lax.broadcasted_iota(jnp.int32, (TILE, TILE), 1)

    def tile(start, length, i, tiles):
        q_at = pl.multiple_of(start + i * TILE, BLK)
        q_tile = q_t[:, pl.ds(q_at, TILE)]

        def step(j, carried, diagonal):
            run_max, run_sum, acc = carried
            k_at = pl.multiple_of(start + j * TILE, BLK)
            scores = dot_f32(keys[pl.ds(k_at, TILE), :], q_tile) * scale
            if diagonal:
                scores = jnp.where(row <= col, scores, masked_score)
            new_max = jnp.maximum(run_max, jnp.max(scores, axis=0, keepdims=True))
            factor = jnp.exp2(run_max - new_max)
            weights = jnp.exp2(scores - new_max)
            run_sum = run_sum * factor + jnp.sum(weights, axis=0, keepdims=True)
            acc = acc * factor + dot_f32(v_t[:, pl.ds(k_at, TILE)], weights.astype(bf16))
            return new_max, run_sum, acc

        carried = (
            jnp.full((1, TILE), masked_score, f32),
            jnp.zeros((1, TILE), f32),
            jnp.zeros((HD, TILE), f32),
        )
        carried = lax.fori_loop(0, i, lambda j, c: step(j, c, False), carried)
        run_max, run_sum, acc = step(i, carried, True)
        lse_ref[:, pl.ds(q_at, TILE)] = jnp.broadcast_to(run_max + jnp.log2(run_sum), (8, TILE))
        seq_out_ref[:, pl.ds(q_at, TILE)] = (acc / run_sum).astype(bf16)

    each_query_tile(seq_ref, rank_ref, seq_count, split, tile)
    for s in range(slots):
        for b in range(subs):
            where = pl.multiple_of(place_ref[s * subs + b] * BLK, BLK)
            outs[s, :, b * BLK : (b + 1) * BLK] = seq_out_ref[:, pl.ds(where, BLK)]


def backward_kernel(seq_count, slots, subs, split, place_ref, seq_ref, rank_ref, *refs):
    parts, grads, lse_ref, seq_out_ref, cos_ref, sin_ref, outs = refs[:7]
    k_t, q_up, g_down, kv, q_left, g_right, row_dot, dq_t, dkv = refs[7:]
    tokens = slots * subs * BLK
    tail = k_t.shape[1] - tokens
    q_up[HD:, :] = jnp.zeros((HD, tokens + tail), bf16)
    g_down[:HD, :] = jnp.zeros((HD, tokens + tail), bf16)
    k_t[:, pl.ds(tokens, tail)] = jnp.zeros((HD, tail), bf16)
    q_up[:HD, pl.ds(tokens, tail)] = jnp.zeros((HD, tail), bf16)
    g_down[HD:, pl.ds(tokens, tail)] = jnp.zeros((HD, tail), bf16)
    row_dot[:, pl.ds(tokens, tail)] = jnp.zeros((8, tail), f32)
    for wide in (kv, q_left, g_right):
        wide[pl.ds(tokens, tail), :] = jnp.zeros((tail, 2 * HD), bf16)
    dq_t[...] = jnp.zeros(dq_t.shape, f32)
    dkv[...] = jnp.zeros(dkv.shape, f32)
    left = lax.broadcasted_iota(jnp.int32, (BLK, 2 * HD), 1) < HD
    for s in range(slots):
        for b in range(subs):
            where = pl.multiple_of(place_ref[s * subs + b] * BLK, BLK)
            cols = slice(b * BLK, (b + 1) * BLK)
            at = pl.ds(where, BLK)
            q_blk = parts[s, 0:HD, cols]
            g_blk = grads[s, :, cols]
            q_up[:HD, at] = q_blk
            g_down[HD:, at] = g_blk
            k_t[:, at] = parts[s, HD : 2 * HD, cols]
            kv[at, :] = flip(parts[s, HD:, cols])
            both = jnp.transpose(jnp.concatenate([q_blk.astype(f32), g_blk.astype(f32)], axis=0))
            q_left[at, :] = jnp.where(left, both, 0.0).astype(bf16)
            g_right[at, :] = jnp.where(left, 0.0, both).astype(bf16)
            dots = jnp.sum(
                g_blk.astype(f32) * seq_out_ref[:, at].astype(f32), axis=0, keepdims=True
            )
            row_dot[:, at] = jnp.broadcast_to(dots, (8, BLK))
    scale = HD ** (-0.5)
    row = lax.broadcasted_iota(jnp.int32, (TILE, TILE), 0)
    col = lax.broadcasted_iota(jnp.int32, (TILE, TILE), 1)
    lane = lax.broadcasted_iota(jnp.int32, (1, TILE), 1)

    def pair(start, length, i, j, diagonal):
        q_at = pl.ds(pl.multiple_of(start + i * TILE, BLK), TILE)
        k_at = pl.ds(pl.multiple_of(start + j * TILE, BLK), TILE)
        lse = jnp.where(i * TILE + lane < length, lse_ref[0:1, q_at], far_score)
        kv_tile = kv[k_at, :]
        scores = dot_f32(kv_tile, q_up[:, q_at]) * (scale * log2e)
        if diagonal:
            scores = jnp.where(row <= col, scores, masked_score)
        probs = jnp.exp2(scores - lse)
        grad_probs = dot_f32(kv_tile, g_down[:, q_at])
        grad_scores = (probs * (grad_probs - row_dot[0:1, q_at])).astype(bf16)
        probs = probs.astype(bf16)
        dkv[k_at, :] += dot_f32(grad_scores, q_left[q_at, :]) + dot_f32(probs, g_right[q_at, :])
        return dot_f32(k_t[:, k_at], grad_scores)

    def tile(start, length, i, tiles):
        total = pair(start, length, i, i, True)
        total = lax.fori_loop(
            0, i, lambda j, c: c + pair(start, length, i, j, False), total
        )
        dq_t[:, pl.ds(pl.multiple_of(start + i * TILE, BLK), TILE)] = total

    each_query_tile(seq_ref, rank_ref, seq_count, split, tile)

    def unrotate(head_block, cosine, sine):
        lower = head_block[:HALF]
        upper = head_block[HALF:ROT]
        return jnp.concatenate(
            [
                lower * cosine + upper * sine,
                upper * cosine - lower * sine,
                head_block[ROT:],
            ],
            axis=0,
        )

    for s in range(slots):
        for b in range(subs):
            where = pl.multiple_of(place_ref[s * subs + b] * BLK, BLK)
            at = pl.ds(where, BLK)
            first = pl.multiple_of(place_ref[slots * subs + s * subs + b] * BLK, BLK)
            cosine = cos_ref[:, pl.ds(first, BLK)]
            sine = sin_ref[:, pl.ds(first, BLK)]
            cols = slice(b * BLK, (b + 1) * BLK)
            outs[s, 0:HD, cols] = unrotate(dq_t[:, at] * scale, cosine, sine).astype(bf16)
            pair_t = jnp.transpose(dkv[at, :])
            outs[s, HD : 2 * HD, cols] = unrotate(pair_t[:HD] * scale, cosine, sine).astype(bf16)
            outs[s, 2 * HD :, cols] = pair_t[HD:].astype(bf16)


def whole_vmem(count):
    return [pl.BlockSpec(memory_space=pltpu.VMEM)] * count


def attention_forward(place, seq, rank, parts, split):
    slots, unused, local_tokens = parts.shape
    tokens = slots * local_tokens
    padded = tokens + TILE
    pairs = tokens * tokens // 2
    return pl.pallas_call(
        functools.partial(forward_kernel, seq.shape[1], slots, local_tokens // BLK, split),
        name="attention_forward",
        out_shape=[
            jax.ShapeDtypeStruct((slots, HD, local_tokens), bf16),
            jax.ShapeDtypeStruct((8, padded), f32),
            jax.ShapeDtypeStruct((HD, padded), bf16),
        ],
        grid_spec=pltpu.PrefetchScalarGridSpec(
            num_scalar_prefetch=3,
            grid=(),
            in_specs=whole_vmem(1),
            out_specs=whole_vmem(3),
            scratch_shapes=[
                pltpu.VMEM((HD, padded), bf16),
                pltpu.VMEM((padded, HD), bf16),
                pltpu.VMEM((HD, padded), bf16),
            ],
        ),
        compiler_params=pltpu.CompilerParams(vmem_limit_bytes=60 * 2**20),
        cost_estimate=pl.CostEstimate(
            flops=16 * pairs * HD, bytes_accessed=tokens * HD * 12, transcendentals=pairs
        ),
    )(place, seq, rank, parts)


def attention_backward(place, seq, rank, parts, grads, lse, seq_out, cosine, sine, split):
    slots, unused, local_tokens = parts.shape
    tokens = slots * local_tokens
    padded = tokens + TILE
    pairs = tokens * tokens // 2
    return pl.pallas_call(
        functools.partial(backward_kernel, seq.shape[1], slots, local_tokens // BLK, split),
        name="attention_backward",
        out_shape=jax.ShapeDtypeStruct((slots, 3 * HD, local_tokens), bf16),
        grid_spec=pltpu.PrefetchScalarGridSpec(
            num_scalar_prefetch=3,
            grid=(),
            in_specs=whole_vmem(6),
            out_specs=whole_vmem(1)[0],
            scratch_shapes=[
                pltpu.VMEM((HD, padded), bf16),
                pltpu.VMEM((2 * HD, padded), bf16),
                pltpu.VMEM((2 * HD, padded), bf16),
                pltpu.VMEM((padded, 2 * HD), bf16),
                pltpu.VMEM((padded, 2 * HD), bf16),
                pltpu.VMEM((padded, 2 * HD), bf16),
                pltpu.VMEM((8, padded), f32),
                pltpu.VMEM((HD, padded), f32),
                pltpu.VMEM((padded, 2 * HD), f32),
            ],
        ),
        compiler_params=pltpu.CompilerParams(vmem_limit_bytes=62 * 2**20),
        cost_estimate=pl.CostEstimate(
            flops=40 * pairs * HD, bytes_accessed=tokens * HD * 24, transcendentals=pairs
        ),
    )(place, seq, rank, parts, grads, lse, seq_out, cosine, sine)


def swap(value, axis, size, offset):
    return lax.ppermute(value, axis, [(i, i ^ offset) for i in range(size)])


def axis_bits(size):
    return [1 << k for k in range(size.bit_length() - 1)]


def all_sum(value, axis, size):
    for bit in axis_bits(size):
        value = value + swap(value, axis, size, bit)
    return value


def slot_order(bits):
    if not bits:
        return [0]
    rest = slot_order(bits[1:])
    return [s | bits[0] for s in rest] + rest


def product_kernel(lhs_dim, rhs_dim, cuts, with_add, order_ref, lhs_ref, rhs_ref, *refs):
    step = pl.program_id(0)
    piece = lax.dot_general(
        lhs_ref[...], rhs_ref[...], (((lhs_dim,), (rhs_dim,)), ((), ())), preferred_element_type=f32
    )
    if with_add:
        piece = piece + refs[0][...].astype(f32)
    piece = piece.astype(bf16)
    outs = refs[1:] if with_add else refs
    for out, first, count in zip(outs, cuts, cuts[1:] + [None]):
        if len(outs) == 1:
            out[...] = piece
        else:
            inside = step >= first if count is None else (step >= first) & (step < count)

            @pl.when(inside)
            def _(out=out):
                out[...] = piece


def piece_products(owners, lhs, rhs, lhs_dim, rhs_dim, columns, half, added, cuts):
    steps = owners[0].shape[0]
    size = owners[1]
    rows = lhs.shape[1 - lhs_dim] // size
    tokens = lhs.shape[lhs_dim]
    table = owners[0].astype(jnp.int32)
    if added is not None:
        table = jnp.concatenate([table, jnp.array(added[1], jnp.int32)])
    lhs_block = (tokens, rows) if lhs_dim == 0 else (rows, tokens)
    rhs_block = (tokens, columns) if rhs_dim == 0 else (columns, tokens)
    in_specs = [
        pl.BlockSpec(lhs_block, (lambda i, t: (0, t[i])) if lhs_dim == 0 else (lambda i, t: (t[i], 0))),
        pl.BlockSpec(rhs_block, (lambda i, t: (0, half)) if rhs_dim == 0 else (lambda i, t: (half, 0))),
    ]
    operands = [lhs, rhs]
    if added is not None:
        in_specs.append(pl.BlockSpec((rows, columns), lambda i, t: (t[steps + i], half)))
        operands.append(added[0])
    ends = cuts[1:] + [steps]
    out_specs = [
        pl.BlockSpec(
            (rows, columns),
            lambda i, t, first=first, last=end - 1: (jnp.clip(i, first, last) - first, 0),
        )
        for first, end in zip(cuts, ends)
    ]
    return pl.pallas_call(
        functools.partial(product_kernel, lhs_dim, rhs_dim, cuts, added is not None),
        name="piece_products",
        out_shape=[
            jax.ShapeDtypeStruct((rows * (end - first), columns), bf16)
            for first, end in zip(cuts, ends)
        ],
        grid_spec=pltpu.PrefetchScalarGridSpec(
            num_scalar_prefetch=1, grid=(steps,), in_specs=in_specs, out_specs=out_specs
        ),
        compiler_params=pltpu.CompilerParams(vmem_limit_bytes=48 * 2**20),
        cost_estimate=pl.CostEstimate(
            flops=2 * steps * rows * columns * tokens,
            bytes_accessed=2 * (steps * rows * (tokens + columns * 2) + columns * tokens),
            transcendentals=0,
        ),
    )(table, *operands)


def halves_orders(size):
    upper = axis_bits(size)[1:]
    return [(upper, slot_order(upper)), (upper[::-1], slot_order(upper[::-1]))]


def piece_sums(index, size, lhs, rhs, lhs_dim, rhs_dim):
    orders = halves_orders(size)
    columns = rhs.shape[1 - rhs_dim]
    if lhs_dim == 0 and (lhs.shape[1] // size) % LANES:
        lhs, lhs_dim = jnp.transpose(lhs), 1
    first_order = orders[0][1]
    far = index ^ jnp.array([s | 1 for s in first_order], jnp.int32)
    sent = piece_products((far, size), lhs, rhs, lhs_dim, rhs_dim, columns, 0, None, [0])[0]
    got = swap(sent, "dp", size, 1)
    pieces = []
    for half, (bits, order) in enumerate(orders):
        near = index ^ jnp.array(order, jnp.int32)
        rows_at = [first_order.index(s) for s in order]
        send, keep = piece_products(
            (near, size), lhs, rhs, lhs_dim, rhs_dim, columns // 2, half, (got, rows_at),
            [0, size // 4],
        )
        for bit in bits:
            got_piece = swap(send, "dp", size, bit)
            cut = keep.shape[0] // 2
            if bit == bits[-1]:
                keep = (keep.astype(f32) + got_piece.astype(f32)).astype(bf16)
            else:
                send = (keep[:cut].astype(f32) + got_piece[:cut].astype(f32)).astype(bf16)
                keep = (keep[cut:].astype(f32) + got_piece[cut:].astype(f32)).astype(bf16)
        pieces.append(keep)
    return pieces


def spread_kernel(quarter, parts, table_ref, *refs):
    ins, out = refs[:-1], refs[-1]
    step = pl.program_id(0)
    for j, piece in enumerate(ins):

        @pl.when(step // quarter == j)
        def _(piece=piece):
            if parts == 1:
                out[...] = piece[...].astype(f32)
            else:
                wide = piece.shape[1] // parts
                for c in range(parts):
                    out[:, c, :] = piece[:, c * wide : (c + 1) * wide].astype(f32)


def spread(index, size, pieces, parts):
    arrays, slots = [], []
    for (bits, unused), piece in zip(halves_orders(size), pieces):
        have, have_slots = piece, [0]
        for bit in bits[:0:-1]:
            have = jnp.concatenate([have, swap(have, "dp", size, bit)], axis=0)
            have_slots = have_slots + [s | bit for s in have_slots]
        other = swap(have, "dp", size, bits[0])
        other_slots = [s | bits[0] for s in have_slots]
        arrays += [have, other, swap(have, "dp", size, 1), swap(other, "dp", size, 1)]
        slots += have_slots + other_slots
        slots += [s | 1 for s in have_slots] + [s | 1 for s in other_slots]
    table = index ^ jnp.array(slots, jnp.int32)
    quarter = size // 4
    rows, columns = pieces[0].shape
    in_specs = [
        pl.BlockSpec(
            (rows, columns),
            lambda i, t, at=j * quarter: (jnp.clip(i - at, 0, quarter - 1), 0),
        )
        for j in range(8)
    ]
    if parts == 1:
        out_shape = (rows * size, 2 * columns)
        out_spec = pl.BlockSpec((rows, columns), lambda i, t: (t[i], i // size))
    else:
        out_shape = (rows * size, parts, 2 * columns // parts)
        out_spec = pl.BlockSpec(
            (rows, parts, columns // parts), lambda i, t: (t[i], 0, i // size)
        )
    return pl.pallas_call(
        functools.partial(spread_kernel, quarter, parts),
        name="spread",
        out_shape=jax.ShapeDtypeStruct(out_shape, f32),
        grid_spec=pltpu.PrefetchScalarGridSpec(
            num_scalar_prefetch=1, grid=(2 * size,), in_specs=in_specs, out_specs=out_spec
        ),
        compiler_params=pltpu.CompilerParams(vmem_limit_bytes=48 * 2**20),
        cost_estimate=pl.CostEstimate(
            flops=0, bytes_accessed=rows * columns * size * 12, transcendentals=0
        ),
    )(table, *arrays)


def local(
    dp_size,
    hidden_in,
    gain,
    bias,
    w_qkv,
    b_qkv,
    w_dense,
    b_dense,
    w_fc1,
    b_fc1,
    w_fc2,
    b_fc2,
    cotangent,
    seq_lengths,
    padding,
    block_perm,
):
    tok_local, dim_local = hidden_in.shape
    model_width = gain.shape[0]
    heads = w_qkv.shape[2] // HD
    split = dp_size // heads
    subs = tok_local // BLK
    nblk = block_perm.shape[0]
    data_index = lax.axis_index("dp")
    tensor_index = lax.axis_index("tensor")
    pos_all, valid_all = token_table(seq_lengths, padding, block_perm)
    my_pos = lax.dynamic_slice_in_dim(pos_all, data_index * tok_local, tok_local)
    my_valid = lax.dynamic_slice_in_dim(valid_all, data_index * tok_local, tok_local)
    cosine, sine = rotary_tables(my_pos)
    cosine_all, sine_all = rotary_tables(jnp.arange(nblk * BLK, dtype=jnp.int32))
    place = jnp.concatenate([block_perm, pos_all[::BLK] // BLK])
    seq = jnp.stack([jnp.cumsum(seq_lengths) - seq_lengths, seq_lengths])
    rank = (data_index // heads).reshape(1).astype(jnp.int32)

    def to_heads(stacked):
        stacked = jnp.concatenate([stacked] * split) if split > 1 else stacked
        return lax.all_to_all(stacked, "dp", 0, 0, tiled=True)

    def to_tokens(stacked):
        got = lax.all_to_all(stacked, "dp", 0, 0, tiled=True)
        if split > 1:
            got = got.reshape(split, heads, *got.shape[1:]).astype(f32)
            got = jnp.sum(got, axis=0).astype(bf16)
        return got

    full_in = lax.all_gather(hidden_in.astype(bf16), "tensor", axis=1, tiled=True).astype(f32)
    grad_proj = lax.all_gather(cotangent.astype(bf16), "tensor", axis=1, tiled=True)
    row_mean = jnp.mean(full_in, axis=-1, keepdims=True)
    centered = full_in - row_mean
    inv_std = lax.rsqrt(jnp.mean(centered * centered, axis=-1, keepdims=True) + epsilon)
    normal_x = centered * inv_std
    normed = (normal_x * gain + bias).astype(bf16)
    projections = (
        jnp.einsum("td,dcf->cft", normed, w_qkv, preferred_element_type=f32) + b_qkv[:, :, None]
    ).reshape(3, heads, HD, tok_local)
    turned = projections[:2, :, :ROT].reshape(2, heads, 2, HALF, tok_local)
    lower, upper = turned[:, :, 0], turned[:, :, 1]
    rotated = jnp.concatenate(
        [
            lower * cosine - upper * sine,
            upper * cosine + lower * sine,
            projections[:2, :, ROT:],
        ],
        axis=2,
    )
    packed = jnp.concatenate([rotated[0], rotated[1], projections[2]], axis=1).astype(bf16)
    parts = to_heads(packed)
    out_stack, lse, seq_out = attention_forward(place, seq, rank, parts, split)
    attended = to_tokens(out_stack).reshape(heads * HD, tok_local)

    hidden_pre = jnp.dot(normed, w_fc1, preferred_element_type=f32) + b_fc1
    activated = gelu_tanh(hidden_pre).astype(bf16)
    partial_value = jnp.einsum(
        "et,ed->td", attended, w_dense, preferred_element_type=f32
    ) + jnp.dot(activated, w_fc2, preferred_element_type=f32)
    projected = lax.psum_scatter(
        partial_value.astype(bf16), "tensor", scatter_dimension=1, tiled=True
    ).astype(f32)
    branch = projected + b_dense + b_fc2
    output = hidden_in + branch
    valid_rows = my_valid.astype(f32)[:, None]
    sum_output = jnp.sum(output * output * valid_rows)
    sum_branch = jnp.sum(branch * branch * valid_rows)
    valid_count = jnp.sum(valid_all.astype(f32)) * model_width

    grad_attended = jnp.einsum(
        "ed,td->et", w_dense, grad_proj, preferred_element_type=f32
    ).astype(bf16)
    grad_stack = to_heads(grad_attended.reshape(heads, HD, tok_local))
    grad_act = jnp.einsum("td,fd->tf", grad_proj, w_fc2, preferred_element_type=f32)
    unused_value, gelu_back = jax.vjp(gelu_tanh, hidden_pre)
    grad_hidden = gelu_back(grad_act)[0].astype(bf16)
    grad_b_fc1 = jnp.sum(grad_hidden.astype(f32), axis=0)
    grad_normed = jnp.einsum("tf,df->td", grad_hidden, w_fc1, preferred_element_type=f32)

    def weight_sum(lhs, rhs, lhs_dim, rhs_dim, parts_out):
        pieces = piece_sums(data_index, dp_size, lhs, rhs, lhs_dim, rhs_dim)
        return spread(data_index, dp_size, pieces, parts_out)

    grad_w_fc2 = weight_sum(activated, grad_proj, 0, 0, 1)
    grad_w_fc1 = weight_sum(normed, grad_hidden, 0, 0, 1)
    grad_w_dense = weight_sum(attended, grad_proj, 1, 0, 1)

    early = jnp.concatenate(
        [jnp.sum(cotangent, axis=0), grad_b_fc1, sum_output[None], sum_branch[None]]
    )
    early = all_sum(early, "dp", dp_size)
    totals = all_sum(early[-2:], "tensor", model_width // dim_local)

    grad_pieces = attention_backward(
        place, seq, rank, parts, grad_stack, lse, seq_out, cosine_all, sine_all, split
    )
    grad_qkv = to_tokens(grad_pieces).reshape(heads, 3, HD, tok_local)
    grad_b_qkv = jnp.transpose(jnp.sum(grad_qkv.astype(f32), axis=3), (1, 0, 2))
    by_half = jnp.transpose(
        grad_qkv.reshape(2, heads // 2, 3, HD, tok_local), (0, 2, 1, 3, 4)
    ).reshape(3 * heads * HD, tok_local)
    grad_w_qkv = weight_sum(normed, by_half, 0, 1, 3)
    grad_normed = grad_normed + jnp.einsum(
        "hcet,dche->td",
        grad_qkv,
        w_qkv.reshape(model_width, 3, heads, HD),
        preferred_element_type=f32,
    )
    grad_local = lax.psum_scatter(
        grad_normed.astype(bf16), "tensor", scatter_dimension=1, tiled=True
    ).astype(f32)
    scaled = grad_normed * gain
    mean_sums = jnp.stack([jnp.sum(scaled, axis=1), jnp.sum(scaled * normal_x, axis=1)])
    mean_sums = all_sum(mean_sums, "tensor", model_width // dim_local) / model_width
    mean_one, mean_two = mean_sums[0][:, None], mean_sums[1][:, None]
    gain_local = lax.dynamic_slice_in_dim(gain, tensor_index * dim_local, dim_local)
    normal_local = lax.dynamic_slice_in_dim(normal_x, tensor_index * dim_local, dim_local, 1)
    grad_input = cotangent + inv_std * (
        grad_local * gain_local - mean_one - normal_local * mean_two
    )
    late = jnp.concatenate(
        [
            jnp.sum(grad_local * normal_local, axis=0),
            jnp.sum(grad_local, axis=0),
            grad_b_qkv.reshape(-1),
        ]
    )
    late = all_sum(late, "dp", dp_size)
    rms = jnp.sqrt(totals / valid_count)
    bias_grad = early[:dim_local]
    return (
        output,
        grad_input,
        late[:dim_local],
        late[dim_local : 2 * dim_local],
        grad_w_qkv,
        late[2 * dim_local :].reshape(3, heads * HD),
        grad_w_dense,
        bias_grad,
        grad_w_fc1,
        early[dim_local:-2],
        grad_w_fc2,
        bias_grad,
        rms[0],
        rms[1],
    )


def solution(mesh):
    return jax.shard_map(
        functools.partial(local, mesh.shape["dp"]),
        mesh=mesh,
        in_specs=(
            P("dp", "tensor"),
            P(),
            P(),
            P(None, None, "tensor"),
            P(None, "tensor"),
            P("tensor", None),
            P("tensor"),
            P(None, "tensor"),
            P("tensor"),
            P("tensor", None),
            P("tensor"),
            P("dp", "tensor"),
            P(),
            P(),
            P(),
        ),
        out_specs=(
            P("dp", "tensor"),
            P("dp", "tensor"),
            P("tensor"),
            P("tensor"),
            P(None, None, "tensor"),
            P(None, "tensor"),
            P("tensor", None),
            P("tensor"),
            P(None, "tensor"),
            P("tensor"),
            P("tensor", None),
            P("tensor"),
            P(),
            P(),
        ),
        check_vma=False,
    )
```

time: 1510 us -> 724 us (0.48)
  matrix products: 590 us -> 77.6 us
  waiting for transfers between devices: 530 us -> 269 us
  Pallas kernels: 0 us -> 190 us
  other arithmetic: 183 us -> 48.4 us
  blocking collectives: 69.9 us -> 0 us
  starting transfers between devices: 0.89 us -> 61.3 us
  local copies, waits for them, and re-layouts: 98 us -> 48.8 us
    dot_general x68 -> x8, matrix products: 590 us -> 77.6 us  [the longest x1 15.3 us: local(): jnp.einsum('td,fd->tf', grad_proj, w_fc2, preferred_element_type=f32)]
    psum x2 -> x0, waiting for transfers between devices: 349 us -> none  [the longest x1 276 us: local(): lax.psum(grad_w_qkv.astype(jnp.bfloat16), 'dp').astype(jnp.float32)]
    pallas_call x0 -> x18, Pallas kernels: none -> 190 us  [the longest x12 67.6 us: piece_products(): pl.pallas_call(functools.partial(product_kernel, lhs_dim, rhs_dim, cuts,...]
    ppermute x0 -> x62, waiting for transfers between devices: none -> 171 us  [swap(): return lax.ppermute(value, axis, [(i, i ^ offset) for i in range(size)])]
    reduce_sum x13 -> x4, other arithmetic: 92.2 us -> 10.6 us  [the longest x1 3.93 us: local(): sum_branch = jnp.sum(branch * branch * valid_rows)]
    psum x2 -> x0, blocking collectives: 69.9 us -> none  [the longest x1 44.3 us: local(): lax.psum((jnp.sum(output * output * valid_rows), jnp.sum(branch * branch...]
    dynamic_slice x65 -> x0, local copies, waits for them, and re-layouts: 58.6 us -> none  [the longest x16 12.4 us: piece_scores(): key_pos = lax.dynamic_slice_in_dim(pos_all, row_start, row_count)]
    all_gather x4 -> x2, waiting for transfers between devices: 144 us -> 95.2 us  [the longest x1 51.7 us: local(): lax.all_gather(hidden_in.astype(bf16), 'tensor', axis=1, tiled=True)]
  transfers between devices with their start and end apart: 8 -> 70, of which waited for: 7 -> 21; matrix products, arithmetic and copies ran while one was open for 28% -> 20% of each run, Pallas kernels for 0% -> 21%
where the time goes in v1:
time: 724 us; the launch traced here: 712 us
  waiting for transfers between devices  269 us (37%)
  Pallas kernels  190 us (26%)
  matrix products  77.6 us (11%)
  starting transfers between devices  61.3 us (8%)
  local copies, waits for them, and re-layouts  48.8 us (7%)
  other arithmetic  48.4 us (7%)
  between operations  15.9 us (2%)
    ppermute x62, waiting for transfers between devices, swap(): return lax.ppermute(value, axis, [(i, i ^ offset) for i in range(size)])  171 us
    pallas_call x12, Pallas kernels, piece_products(): pl.pallas_call(functools.partial(product_kernel, lhs_dim, rhs_dim, cuts,...  67.6 us
    pallas_call x4, Pallas kernels, spread(): pl.pallas_call(functools.partial(spread_kernel, quarter, parts), name='sp...  51.8 us
    all_gather x1, waiting for transfers between devices, local(): lax.all_gather(hidden_in.astype(bf16), 'tensor', axis=1, tiled=True)  51.7 us
    all_gather x1, waiting for transfers between devices, local(): lax.all_gather(cotangent.astype(bf16), 'tensor', axis=1, tiled=True)  43.5 us
    ppermute x62, starting transfers between devices, swap(): return lax.ppermute(value, axis, [(i, i ^ offset) for i in range(size)])  43.4 us
    unnamed x135, local copies, waits for them, and re-layouts  42.3 us
    pallas_call x1, Pallas kernels, attention_backward(): pl.pallas_call(functools.partial(backward_kernel, seq.shape[1], slots, lo...  40.3 us
  transfers between devices with their start and end apart: 70, of which 21 were waited for; matrix products, arithmetic and copies ran while one was open for 20% of the time, Pallas kernels for 21%

profile of v1, /device:TPU:0, one launch (start us, length us, event | category | flops | bytes accessed | tf_op | source)
XLA Modules:
  0.0 711.8 jit_solution(9723594884377519301)
XLA Ops:
  12.7 8.8 %copy.71 = bf16[2048,3,512]{0,2,1:T(8,128)(2,1)} copy(bf16[2048,3,512]{2,0,1:T(8,128)(2,1)} %param.42) | data formatting | bytes 12582912 | tf_op args[3]
  24.6 51.7 %all-gather.3.cloned.1.call-done = bf16[768,2048]{1,0:T(8,128)(2,1)} async-done(((bf16[768,512]{1,0:T(8,128)(2,1)}), bf16[768,2048]{1,0:T(8,128)(2,1)}) %all-gather.3.cloned.1.call-update) | async-done | bytes 3145744 | tf_op jit(solution)/shard_map/all_gather | solution.py:519
  81.4 8.8 %broadcast_add_fusion = f32[768,3,512]{0,2,1:T(8,128)S(1)} fusion(f32[3,512]{1,0:T(4,128)S(1)} %copy-done.60, bf16[2048,3,512]{2,0,1:T(8,128)(2,1)} %param.42, bf16[768,2048]{1,0:T(8,128)(2,1)S(1)} %add_convert_fusion.1.lhs_ref), kind=kOutput, calls=%fused_computation.30 | convolution fusion | flops 4833017856 | bytes 14161920 | tf_op jit(solution)/shard_map/td,dcf->cft/dot_general | solution.py:527
  92.6 4.6 all-to-all-start
  97.2 43.5 %all-gather.5.cloned.1.call-done.rhs_ref = bf16[768,2048]{1,0:T(8,128)(2,1)} async-done(((bf16[768,512]{1,0:T(8,128)(2,1)}), bf16[768,2048]{1,0:T(8,128)(2,1)}) %all-gather.5.cloned.1.call-update) | async-done | bytes 3145744 | tf_op jit(solution)/shard_map/all_gather | solution.py:520
  140.6 5.2 convolution_convert_fusion
  145.9 10.7 %fusion.30 = f32[768,2048]{1,0:T(8,128)} fusion(bf16[768,2048]{1,0:T(8,128)(2,1)S(1)} %add_convert_fusion.1.lhs_ref, bf16[2048,2048]{1,0:T(8,128)(2,1)} %param.46), kind=kOutput, calls=%fused_computation.126 | convolution fusion | flops 6442450944 | bytes 17825792 | tf_op jit(solution)/shard_map/dot_general | solution.py:544
  156.6 3.7 all-to-all-start.2
  160.2 30.7 %attention_forward.1 = (bf16[8,64,768]{2,1,0:T(8,128)(2,1)}, f32[8,6656]{1,0:T(8,128)}, bf16[64,6656]{1,0:T(8,128)(2,1)}) custom-call(s32[96]{0:T(128)} %pad_add_fusion.1.place_ref, s32[2,3]{1,0:T(2,128)} %pad_add_fusion.seq_ref, s32[1]{0:T(128)} %bitcast.5.rank_ref, bf16[8,192,768]{2,1,0:T(8,128)(2,1)} %all-to-all-done.refs_0_), custom_call_target="tpu_custom_call" | custom-call | flops 19327352832 | bytes 4718592 | tf_op jit(solution)/shard_map/attention_forward/pallas_call | solution.py:235
  191.8 40.3 %attention_backward.1 = bf16[8,192,768]{2,1,0:T(8,128)(2,1)} custom-call(s32[96]{0:T(128)} %pad_add_fusion.1.place_ref, s32[2,3]{1,0:T(2,128)} %pad_add_fusion.seq_ref, s32[1]{0:T(128)} %bitcast.5.rank_ref, bf16[8,192,768]{2,1,0:T(8,128)(2,1)} %all-to-all-done.refs_0_, bf16[8,64,768]{2,1,0:T(8,128)(2,1)} %copy-done.37, f32[8,6656]{1,0:T(8,128)} %get-tuple-element.34.refs_2_, ...), custom_call_target="tpu_custom_call" | custom-call | flops 48318382080 | bytes 9437184 | tf_op jit(solution)/shard_map/attention_backward/pallas_call | solution.py:266
  232.1 4.6 all-to-all-start.3
  237.2 15.3 %convert_reduce_fusion.1 = (f32[2048]{0:T(1024)S(1)}, bf16[768,2048]{1,0:T(8,128)(2,1)S(1)}, bf16[768,2048]{1,0:T(8,128)(2,1)}) fusion(f32[768,2048]{1,0:T(8,128)} %fusion.30, f32[2048]{0:T(1024)S(1)} %copy-done.61, bf16[768,2048]{1,0:T(8,128)(2,1)S(1)} %copy-done.3, bf16[2048,2048]{1,0:T(8,128)(2,1)} %param.48), kind=kOutput, calls=%fused_computation.15 | convolution fusion | flops 6481770496 | bytes 24133632 | tf_op jit(solution)/shard_map/td,fd->tf/dot_general | solution.py:563
  254.1 10.9 %fusion.32 = f32[768,2048]{1,0:T(8,128)} fusion(bf16[768,2048]{1,0:T(8,128)(2,1)S(1)} %get-tuple-element.106.rhs_ref, bf16[2048,2048]{1,0:T(8,128)(2,1)} %param.46), kind=kOutput, calls=%fused_computation.128 | convolution fusion | flops 6442450944 | bytes 17825792 | tf_op jit(solution)/shard_map/tf,df->td/dot_general | solution.py:567
  266.2 13.1 %multiply_reduce_fusion.1 = (f32[768]{0:T(1024)S(1)}, f32[768]{0:T(1024)S(1)}, bf16[768,2048]{1,0:T(8,128)(2,1)}, f32[768,2048]{1,0:T(8,128)}) fusion(f32[2048]{0:T(1024)S(1)} %copy-done.43, f32[768]{0:T(1024)S(1)} %add_rsqrt_fusion, f32[768]{0:T(1024)S(1)} %broadcast_multiply_fusion, bf16[768,2048]{1,0:T(8,128)(2,1)S(1)} %copy-done.32, ...), kind=kOutput, calls=%fused_computation.20 | convolution fusion | flops 4845991936 | bytes 27545600 | tf_op jit(solution)/shard_map/hcet,dche->td/dot_general | solution.py:592
  281.2 8.0 %piece_products.18 = bf16[1024,2048]{1,0:T(8,128)(2,1)} custom-call(s32[4]{0:T(128)S(1)} %broadcast_xor_fusion.1.order_ref, bf16[768,2048]{1,0:T(8,128)(2,1)S(1)} %copy-done.1, bf16[768,2048]{1,0:T(8,128)(2,1)} %copy-done.33), custom_call_target="tpu_custom_call" | custom-call | flops 3221225472 | bytes 13107200 | tf_op jit(solution)/shard_map/piece_products/pallas_call | solution.py:361
  289.2 4.2 all-to-all-start.1
  295.7 8.0 %piece_products.21 = bf16[1024,2048]{1,0:T(8,128)(2,1)} custom-call(s32[4]{0:T(128)S(1)} %broadcast_xor_fusion.1.order_ref, bf16[768,2048]{1,0:T(8,128)(2,1)S(1)} %copy-done.5, bf16[768,2048]{1,0:T(8,128)(2,1)} %all-gather.5.cloned.1.call-done.rhs_ref), custom_call_target="tpu_custom_call" | custom-call | flops 3221225472 | bytes 13107200 | tf_op jit(solution)/shard_map/piece_products/pallas_call | solution.py:361
  306.0 4.6 piece_products.15
  310.8 9.0 %fusion.31 = f32[768,2048]{1,0:T(8,128)S(1)} fusion(bf16[768,2048]{1,0:T(8,128)(2,1)S(1)} %copy-done.6, bf16[2048,2048]{1,0:T(8,128)(2,1)} %param.48), kind=kOutput, calls=%fused_computation.127 | convolution fusion | flops 6442450944 | bytes 17825792 | tf_op jit(solution)/shard_map/dot_general | solution.py:548
  319.8 4.5 piece_products.16
  324.9 4.5 piece_products.17
  330.5 4.6 add_convert_fusion
  341.5 6.6 piece_products.12
  348.1 5.4 piece_products.19
  355.1 5.7 piece_products.20
  363.1 5.4 piece_products.22
  370.0 19.0 %collective-permute-done.21 = bf16[64,1024]{1,0:T(8,128)(2,1)S(1)} collective-permute-done((bf16[64,1024]{1,0:T(8,128)(2,1)S(1)}, bf16[64,1024]{1,0:T(8,128)(2,1)S(1)}, u32[]{:S(2)}, u32[]{:S(2)}) %collective-permute-start.21) | collective-permute-done | bytes 131104 | tf_op jit(solution)/shard_map/ppermute | solution.py:295
  390.6 5.7 piece_products.23
  402.6 12.5 %collective-permute-done.48 = bf16[512,1024]{1,0:T(8,128)(2,1)} collective-permute-done((bf16[512,1024]{1,0:T(8,128)(2,1)S(1)}, bf16[512,1024]{1,0:T(8,128)(2,1)}, u32[]{:S(2)}, u32[]{:S(2)}) %collective-permute-start.48) | collective-permute-done | bytes 1048608 | tf_op jit(solution)/shard_map/ppermute | solution.py:295
  417.5 4.9 collective-permute-done.54
  423.0 8.9 %collective-permute-done.36 = bf16[256,1024]{1,0:T(8,128)(2,1)S(1)} collective-permute-done((bf16[256,1024]{1,0:T(8,128)(2,1)S(1)}, bf16[256,1024]{1,0:T(8,128)(2,1)S(1)}, u32[]{:S(2)}, u32[]{:S(2)}) %collective-permute-start.36) | collective-permute-done | bytes 524320 | tf_op jit(solution)/shard_map/ppermute | solution.py:295
  436.2 16.1 %collective-permute-done.28.refs_5_ = bf16[128,1024]{1,0:T(8,128)(2,1)S(1)} collective-permute-done((bf16[128,1024]{1,0:T(8,128)(2,1)S(1)}, bf16[128,1024]{1,0:T(8,128)(2,1)S(1)}, u32[]{:S(2)}, u32[]{:S(2)}) %collective-permute-start.28) | collective-permute-done | bytes 262176 | tf_op jit(solution)/shard_map/ppermute | solution.py:295
  455.8 5.2 collective-permute-done.37
  461.4 4.6 piece_products.13
  466.0 4.6 piece_products.14
  477.6 47.2 %collective-permute-done.56 = bf16[256,1024]{1,0:T(8,128)(2,1)S(1)} collective-permute-done((bf16[256,1024]{1,0:T(8,128)(2,1)S(1)}, bf16[256,1024]{1,0:T(8,128)(2,1)S(1)}, u32[]{:S(2)}, u32[]{:S(2)}) %collective-permute-start.56) | collective-permute-done | bytes 524320 | tf_op jit(solution)/shard_map/ppermute | solution.py:295
  532.4 25.4 %collective-permute-done.7 = bf16[256,768]{1,0:T(8,128)(2,1)} collective-permute-done((bf16[256,768]{1,0:T(8,128)(2,1)}, bf16[256,768]{1,0:T(8,128)(2,1)}, u32[]{:S(2)}, u32[]{:S(2)}) %collective-permute-start.7) | collective-permute-done | bytes 393248 | tf_op jit(solution)/shard_map/ppermute | solution.py:295
  576.3 5.1 collective-permute-done.14
  585.5 6.7 collective-permute-done.57.refs_5_
  594.9 3.9 fusion.19
  599.4 3.9 multiply_reduce_fusion.2
  605.2 4.3 collective-permute-done.9.refs_1_
  624.8 6.6 spread.5
  631.5 14.3 %spread.6 = f32[2048,2048]{1,0:T(8,128)} custom-call(s32[16]{0:T(128)S(1)} %broadcast_xor_fusion.3.table_ref, bf16[512,1024]{1,0:T(8,128)(2,1)S(1)} %pad_maximum_fusion.1.refs_0_, bf16[512,1024]{1,0:T(8,128)(2,1)} %collective-permute-done.38.refs_1_, bf16[512,1024]{1,0:T(8,128)(2,1)S(1)} %copy-done.9, bf16[512,1024]{1,0:T(8,128)(2,1)} %collective-permute-done.40.refs_3_, ...), custom_call_target="tpu_custom_call" | custom-call | bytes 25165824 | tf_op jit(solution)/shard_map/spread/pallas_call | solution.py:459
  645.8 15.4 %spread.7 = f32[2048,2048]{1,0:T(8,128)} custom-call(s32[16]{0:T(128)S(1)} %broadcast_xor_fusion.3.table_ref, bf16[512,1024]{1,0:T(8,128)(2,1)S(1)} %pad_maximum_fusion.3.refs_0_, bf16[512,1024]{1,0:T(8,128)(2,1)} %collective-permute-done.51.refs_1_, bf16[512,1024]{1,0:T(8,128)(2,1)} %collective-permute-done.52.refs_2_, ...), custom_call_target="tpu_custom_call" | custom-call | bytes 25165824 | tf_op jit(solution)/shard_map/spread/pallas_call | solution.py:459
  661.2 15.5 %spread.4 = f32[2048,3,512]{2,1,0:T(4,128)} custom-call(s32[16]{0:T(128)S(1)} %broadcast_xor_fusion.3.table_ref, bf16[512,768]{1,0:T(8,128)(2,1)} %pad_maximum_fusion.5.refs_0_, bf16[512,768]{1,0:T(8,128)(2,1)} %collective-permute-done.9.refs_1_, bf16[512,768]{1,0:T(8,128)(2,1)S(1)} %copy-done.13, bf16[512,768]{1,0:T(8,128)(2,1)} %collective-permute-done.11.refs_3_, ...), custom_call_target="tpu_custom_call" | custom-call | bytes 18874368 | tf_op jit(solution)/shard_map/spread/pallas_call | solution.py:459
  676.6 14.6 %copy.75 = f32[2048,3,512]{2,0,1:T(8,128)} copy(f32[2048,3,512]{2,1,0:T(4,128)} %spread.4) | data formatting | bytes 25165824
  700.0 3.6 collective-permute-done.61
  (350 shorter events, 125.5 us)
Async XLA Ops:
  7.2 69.2 %all-gather.3.cloned.1.call-start = ((), (), s32[]{:S(2)}) async-start(), calls=%async_computation.6 | async-start | bytes 3932160 | tf_op jit(solution)/shard_map/all_gather | solution.py:519
  9.8 130.8 %all-gather.5.cloned.1.call-start = ((), (), s32[]{:S(2)}) async-start(), calls=%async_computation.8 | async-start | bytes 3932160 | tf_op jit(solution)/shard_map/all_gather | solution.py:520
  92.6 64.0 %all-to-all-start = ((bf16[8,192,768]{2,1,0:T(8,128)(2,1)}), bf16[8,192,768]{2,1,0:T(8,128)(2,1)}, u32[]{:S(2)}, u32[]{:S(2)}) async-start(bf16[8,192,768]{2,1,0:T(8,128)(2,1)} %pad_maximum_fusion), calls=%async_computation | async-start | bytes 4718592 | tf_op jit(solution)/shard_map/all_to_all | solution.py:510
  156.6 34.3 %all-to-all-start.2 = ((bf16[8,64,768]{2,1,0:T(8,128)(2,1)}), bf16[8,64,768]{2,1,0:T(8,128)(2,1)S(1)}, u32[]{:S(2)}, u32[]{:S(2)}) async-start(bf16[8,64,768]{2,1,0:T(8,128)(2,1)} %bitcast.80), calls=%async_computation.3 | async-start | bytes 1572864 | tf_op jit(solution)/shard_map/all_to_all | solution.py:510
  232.1 34.1 %all-to-all-start.3 = ((bf16[8,192,768]{2,1,0:T(8,128)(2,1)}), bf16[8,192,768]{2,1,0:T(8,128)(2,1)}, u32[]{:S(2)}, u32[]{:S(2)}) async-start(bf16[8,192,768]{2,1,0:T(8,128)(2,1)} %attention_backward.1), calls=%async_computation.4 | async-start | bytes 4718592 | tf_op jit(solution)/shard_map/all_to_all | solution.py:513
  236.7 358.1 %reduce-scatter.5.cloned.1.call-start = ((), (), s32[]{:S(2)}) async-start(), calls=%async_computation.9 | async-start | bytes 3932160 | tf_op jit(solution)/shard_map/reduce_scatter | solution.py:598
  289.2 58.9 %collective-permute-start.34 = (bf16[1024,2048]{1,0:T(8,128)(2,1)}, bf16[1024,2048]{1,0:T(8,128)(2,1)}, u32[]{:S(2)}, u32[]{:S(2)}) collective-permute-start(bf16[1024,2048]{1,0:T(8,128)(2,1)} %piece_products.18), channel_id=1, source_target_pairs={{0,4},{4,0},{8,12},{12,8},{16,20},{20,16},{24,28},{28,24},{1,5},{5... | collective-permute-start | bytes 12582920 | tf_op jit(solution)/shard_map/ppermute | solution.py:295
  293.4 305.9 %reduce-scatter.3.cloned.1.call-start = ((), (), s32[]{:S(2)}) async-start(), calls=%async_computation.7 | async-start | bytes 3932160 | tf_op jit(solution)/shard_map/reduce_scatter | solution.py:549
  303.8 58.3 %collective-permute-start.47 = (bf16[1024,2048]{1,0:T(8,128)(2,1)}, bf16[1024,2048]{1,0:T(8,128)(2,1)}, u32[]{:S(2)}, u32[]{:S(2)}) collective-permute-start(bf16[1024,2048]{1,0:T(8,128)(2,1)} %piece_products.21), channel_id=1, source_target_pairs={{0,4},{4,0},{8,12},{12,8},{16,20},{20,16},{24,28},{28,24},{1,5},{5... | collective-permute-start | bytes 12582920 | tf_op jit(solution)/shard_map/ppermute | solution.py:295
  338.0 22.8 %collective-permute-start.26 = (bf16[64,1024]{1,0:T(8,128)(2,1)S(1)}, bf16[64,1024]{1,0:T(8,128)(2,1)S(1)}, u32[]{:S(2)}, u32[]{:S(2)}) collective-permute-start(bf16[64,1024]{1,0:T(8,128)(2,1)S(1)} %add_convert_fusion.21), channel_id=1, source_target_pairs={{0,8},{4,12},{8,0},{12,4},{16,24},{20,28},{24,16},{28,20},{1,9},{5... | collective-permute-start | bytes 393224 | tf_op jit(solution)/shard_map/ppermute | solution.py:295
  339.5 28.9 %collective-permute-start = (f32[2,768]{1,0:T(2,128)S(1)}, f32[2,768]{1,0:T(2,128)S(1)}, u32[]{:S(2)}, u32[]{:S(2)}) collective-permute-start(f32[2,768]{1,0:T(2,128)S(1)} %pad_maximum_fusion.10), channel_id=1, source_target_pairs={{0,1},{1,0},{2,3},{3,2},{4,5},{5,4},{6,7},{7,6},{8,9},{9,8},{10,11... | collective-permute-start | bytes 18440 | tf_op jit(solution)/shard_map/ppermute | solution.py:295
  348.1 112.9 %collective-permute-start.5 = (bf16[1024,1536]{1,0:T(8,128)(2,1)}, bf16[1024,1536]{1,0:T(8,128)(2,1)}, u32[]{:S(2)}, u32[]{:S(2)}) collective-permute-start(bf16[1024,1536]{1,0:T(8,128)(2,1)} %piece_products.12), channel_id=1, source_target_pairs={{0,4},{4,0},{8,12},{12,8},{16,20},{20,16},{24,28},{28,24},{1,5},{5... | collective-permute-start | bytes 9437192 | tf_op jit(solution)/shard_map/ppermute | solution.py:295
  353.5 45.3 %collective-permute-start.35 = (bf16[512,1024]{1,0:T(8,128)(2,1)S(1)}, bf16[512,1024]{1,0:T(8,128)(2,1)}, u32[]{:S(2)}, u32[]{:S(2)}) collective-permute-start(bf16[512,1024]{1,0:T(8,128)(2,1)S(1)} %get-tuple-element.45), channel_id=1, source_target_pairs={{0,8},{4,12},{8,0},{12,4},{16,24},{20,28},{24,16},{28,20},{1,9},{5... | collective-permute-start | bytes 3145736 | tf_op jit(solution)/shard_map/ppermute | solution.py:295
  360.8 40.4 %collective-permute-start.41 = (bf16[512,1024]{1,0:T(8,128)(2,1)S(1)}, bf16[512,1024]{1,0:T(8,128)(2,1)S(1)}, u32[]{:S(2)}, u32[]{:S(2)}) collective-permute-start(bf16[512,1024]{1,0:T(8,128)(2,1)S(1)} %get-tuple-element.47), channel_id=1, source_target_pairs={{0,16},{4,20},{8,24},{12,28},{16,0},{20,4},{24,8},{28,12},{1,17},{... | collective-permute-start | bytes 3145736 | tf_op jit(solution)/shard_map/ppermute | solution.py:295
  362.1 26.9 %collective-permute-start.21 = (bf16[64,1024]{1,0:T(8,128)(2,1)S(1)}, bf16[64,1024]{1,0:T(8,128)(2,1)S(1)}, u32[]{:S(2)}, u32[]{:S(2)}) collective-permute-start(bf16[64,1024]{1,0:T(8,128)(2,1)S(1)} %add_convert_fusion.23), channel_id=1, source_target_pairs={{0,16},{4,20},{8,24},{12,28},{16,0},{20,4},{24,8},{28,12},{1,17},{... | collective-permute-start | bytes 393224 | tf_op jit(solution)/shard_map/ppermute | solution.py:295
  368.5 27.8 %collective-permute-start.27 = (bf16[64,1024]{1,0:T(8,128)(2,1)S(1)}, bf16[64,1024]{1,0:T(8,128)(2,1)S(1)}, u32[]{:S(2)}, u32[]{:S(2)}) collective-permute-start(bf16[64,1024]{1,0:T(8,128)(2,1)S(1)} %add_convert_fusion.20), channel_id=1, source_target_pairs={{0,8},{4,12},{8,0},{12,4},{16,24},{20,28},{24,16},{28,20},{1,9},{5... | collective-permute-start | bytes 393224 | tf_op jit(solution)/shard_map/ppermute | solution.py:295
  389.0 26.1 %collective-permute-start.48 = (bf16[512,1024]{1,0:T(8,128)(2,1)S(1)}, bf16[512,1024]{1,0:T(8,128)(2,1)}, u32[]{:S(2)}, u32[]{:S(2)}) collective-permute-start(bf16[512,1024]{1,0:T(8,128)(2,1)S(1)} %get-tuple-element.49), channel_id=1, source_target_pairs={{0,8},{4,12},{8,0},{12,4},{16,24},{20,28},{24,16},{28,20},{1,9},{5... | collective-permute-start | bytes 3145736 | tf_op jit(solution)/shard_map/ppermute | solution.py:295
  396.3 26.1 %collective-permute-start.54 = (bf16[512,1024]{1,0:T(8,128)(2,1)S(1)}, bf16[512,1024]{1,0:T(8,128)(2,1)S(1)}, u32[]{:S(2)}, u32[]{:S(2)}) collective-permute-start(bf16[512,1024]{1,0:T(8,128)(2,1)S(1)} %get-tuple-element.51), channel_id=1, source_target_pairs={{0,16},{4,20},{8,24},{12,28},{16,0},{20,4},{24,8},{28,12},{1,17},{... | collective-permute-start | bytes 3145736 | tf_op jit(solution)/shard_map/ppermute | solution.py:295
  398.8 34.8 %collective-permute-start.1 = (f32[2,768]{1,0:T(2,128)S(1)}, f32[2,768]{1,0:T(2,128)S(1)}, u32[]{:S(2)}, u32[]{:S(2)}) collective-permute-start(f32[2,768]{1,0:T(2,128)S(1)} %fusion.25), channel_id=1, source_target_pairs={{0,2},{1,3},{2,0},{3,1},{4,6},{5,7},{6,4},{7,5},{8,10},{9,11},{10,... | collective-permute-start | bytes 18440 | tf_op jit(solution)/shard_map/ppermute | solution.py:295
  401.3 32.4 %collective-permute-start.22 = (bf16[128,1024]{1,0:T(8,128)(2,1)S(1)}, bf16[128,1024]{1,0:T(8,128)(2,1)S(1)}, u32[]{:S(2)}, u32[]{:S(2)}) collective-permute-start(bf16[128,1024]{1,0:T(8,128)(2,1)S(1)} %pad_maximum_fusion.7.refs_0_), channel_id=1, source_target_pairs={{0,8},{4,12},{8,0},{12,4},{16,24},{20,28},{24,16},{28,20},{1,9},{5... | collective-permute-start | bytes 786440 | tf_op jit(solution)/shard_map/ppermute | solution.py:295
  431.9 20.8 %collective-permute-start.49 = (bf16[256,1024]{1,0:T(8,128)(2,1)S(1)}, bf16[256,1024]{1,0:T(8,128)(2,1)S(1)}, u32[]{:S(2)}, u32[]{:S(2)}) collective-permute-start(bf16[256,1024]{1,0:T(8,128)(2,1)S(1)} %add_convert_fusion.6), channel_id=1, source_target_pairs={{0,16},{4,20},{8,24},{12,28},{16,0},{20,4},{24,8},{28,12},{1,17},{... | collective-permute-start | bytes 1572872 | tf_op jit(solution)/shard_map/ppermute | solution.py:295
  433.7 18.6 %collective-permute-start.28 = (bf16[128,1024]{1,0:T(8,128)(2,1)S(1)}, bf16[128,1024]{1,0:T(8,128)(2,1)S(1)}, u32[]{:S(2)}, u32[]{:S(2)}) collective-permute-start(bf16[128,1024]{1,0:T(8,128)(2,1)S(1)} %pad_maximum_fusion.8.refs_4_), channel_id=1, source_target_pairs={{0,16},{4,20},{8,24},{12,28},{16,0},{20,4},{24,8},{28,12},{1,17},{... | collective-permute-start | bytes 786440 | tf_op jit(solution)/shard_map/ppermute | solution.py:295
  435.4 25.6 %collective-permute-start.37 = (bf16[256,1024]{1,0:T(8,128)(2,1)S(1)}, bf16[256,1024]{1,0:T(8,128)(2,1)S(1)}, u32[]{:S(2)}, u32[]{:S(2)}) collective-permute-start(bf16[256,1024]{1,0:T(8,128)(2,1)S(1)} %add_convert_fusion.11), channel_id=1, source_target_pairs={{0,16},{4,20},{8,24},{12,28},{16,0},{20,4},{24,8},{28,12},{1,17},{... | collective-permute-start | bytes 1572872 | tf_op jit(solution)/shard_map/ppermute | solution.py:295
  436.1 19.6 %collective-permute-start.29 = (bf16[128,1024]{1,0:T(8,128)(2,1)S(1)}, bf16[128,1024]{1,0:T(8,128)(2,1)S(1)}, u32[]{:S(2)}, u32[]{:S(2)}) collective-permute-start(bf16[128,1024]{1,0:T(8,128)(2,1)S(1)} %pad_maximum_fusion.8.refs_4_), channel_id=1, source_target_pairs={{0,4},{4,0},{8,12},{12,8},{16,20},{20,16},{24,28},{28,24},{1,5},{5... | collective-permute-start | bytes 786440 | tf_op jit(solution)/shard_map/ppermute | solution.py:295
  452.3 20.3 %collective-permute-start.55 = (bf16[256,1024]{1,0:T(8,128)(2,1)S(1)}, bf16[256,1024]{1,0:T(8,128)(2,1)S(1)}, u32[]{:S(2)}, u32[]{:S(2)}) collective-permute-start(bf16[256,1024]{1,0:T(8,128)(2,1)S(1)} %add_convert_fusion.3), channel_id=1, source_target_pairs={{0,8},{4,12},{8,0},{12,4},{16,24},{20,28},{24,16},{28,20},{1,9},{5... | collective-permute-start | bytes 1572872 | tf_op jit(solution)/shard_map/ppermute | solution.py:295
  452.7 20.8 %collective-permute-start.43 = (bf16[256,1024]{1,0:T(8,128)(2,1)S(1)}, bf16[256,1024]{1,0:T(8,128)(2,1)S(1)}, u32[]{:S(2)}, u32[]{:S(2)}) collective-permute-start(bf16[256,1024]{1,0:T(8,128)(2,1)S(1)} %add_convert_fusion.8), channel_id=1, source_target_pairs={{0,8},{4,12},{8,0},{12,4},{16,24},{20,28},{24,16},{28,20},{1,9},{5... | collective-permute-start | bytes 1572872 | tf_op jit(solution)/shard_map/ppermute | solution.py:295
  471.4 56.2 %collective-permute-start.38 = (bf16[512,1024]{1,0:T(8,128)(2,1)S(1)}, bf16[512,1024]{1,0:T(8,128)(2,1)}, u32[]{:S(2)}, u32[]{:S(2)}) collective-permute-start(bf16[512,1024]{1,0:T(8,128)(2,1)S(1)} %pad_maximum_fusion.1.refs_0_), channel_id=1, source_target_pairs={{0,8},{4,12},{8,0},{12,4},{16,24},{20,28},{24,16},{28,20},{1,9},{5... | collective-permute-start | bytes 3145736 | tf_op jit(solution)/shard_map/ppermute | solution.py:295
  472.6 55.4 %collective-permute-start.39 = (bf16[512,1024]{1,0:T(8,128)(2,1)S(1)}, bf16[512,1024]{1,0:T(8,128)(2,1)S(1)}, u32[]{:S(2)}, u32[]{:S(2)}) collective-permute-start(bf16[512,1024]{1,0:T(8,128)(2,1)S(1)} %pad_maximum_fusion.1.refs_0_), channel_id=1, source_target_pairs={{0,4},{4,0},{8,12},{12,8},{16,20},{20,16},{24,28},{28,24},{1,5},{5... | collective-permute-start | bytes 3145736 | tf_op jit(solution)/shard_map/ppermute | solution.py:295
  472.6 54.0 %collective-permute-start.6 = (bf16[512,768]{1,0:T(8,128)(2,1)S(1)}, bf16[512,768]{1,0:T(8,128)(2,1)S(1)}, u32[]{:S(2)}, u32[]{:S(2)}) collective-permute-start(bf16[512,768]{1,0:T(8,128)(2,1)S(1)} %get-tuple-element.37), channel_id=1, source_target_pairs={{0,8},{4,12},{8,0},{12,4},{16,24},{20,28},{24,16},{28,20},{1,9},{5... | collective-permute-start | bytes 2359304 | tf_op jit(solution)/shard_map/ppermute | solution.py:295
  473.6 55.5 %collective-permute-start.12 = (bf16[512,768]{1,0:T(8,128)(2,1)S(1)}, bf16[512,768]{1,0:T(8,128)(2,1)S(1)}, u32[]{:S(2)}, u32[]{:S(2)}) collective-permute-start(bf16[512,768]{1,0:T(8,128)(2,1)S(1)} %get-tuple-element.39), channel_id=1, source_target_pairs={{0,16},{4,20},{8,24},{12,28},{16,0},{20,4},{24,8},{28,12},{1,17},{... | collective-permute-start | bytes 2359304 | tf_op jit(solution)/shard_map/ppermute | solution.py:295
  475.6 49.2 %collective-permute-start.56 = (bf16[256,1024]{1,0:T(8,128)(2,1)S(1)}, bf16[256,1024]{1,0:T(8,128)(2,1)S(1)}, u32[]{:S(2)}, u32[]{:S(2)}) collective-permute-start(bf16[256,1024]{1,0:T(8,128)(2,1)S(1)} %add_convert_fusion.2), channel_id=1, source_target_pairs={{0,8},{4,12},{8,0},{12,4},{16,24},{20,28},{24,16},{28,20},{1,9},{5... | collective-permute-start | bytes 1572872 | tf_op jit(solution)/shard_map/ppermute | solution.py:295
  524.8 35.5 %collective-permute-start.44 = (bf16[512,1024]{1,0:T(8,128)(2,1)S(1)}, bf16[512,1024]{1,0:T(8,128)(2,1)}, u32[]{:S(2)}, u32[]{:S(2)}) collective-permute-start(bf16[512,1024]{1,0:T(8,128)(2,1)S(1)} %pad_maximum_fusion.2.refs_4_), channel_id=1, source_target_pairs={{0,16},{4,20},{8,24},{12,28},{16,0},{20,4},{24,8},{28,12},{1,17},{... | collective-permute-start | bytes 3145736 | tf_op jit(solution)/shard_map/ppermute | solution.py:295
  526.6 37.0 %collective-permute-start.45 = (bf16[512,1024]{1,0:T(8,128)(2,1)S(1)}, bf16[512,1024]{1,0:T(8,128)(2,1)}, u32[]{:S(2)}, u32[]{:S(2)}) collective-permute-start(bf16[512,1024]{1,0:T(8,128)(2,1)S(1)} %pad_maximum_fusion.2.refs_4_), channel_id=1, source_target_pairs={{0,4},{4,0},{8,12},{12,8},{16,20},{20,16},{24,28},{28,24},{1,5},{5... | collective-permute-start | bytes 3145736 | tf_op jit(solution)/shard_map/ppermute | solution.py:295
  527.6 40.6 %collective-permute-start.51 = (bf16[512,1024]{1,0:T(8,128)(2,1)S(1)}, bf16[512,1024]{1,0:T(8,128)(2,1)}, u32[]{:S(2)}, u32[]{:S(2)}) collective-permute-start(bf16[512,1024]{1,0:T(8,128)(2,1)S(1)} %pad_maximum_fusion.3.refs_0_), channel_id=1, source_target_pairs={{0,8},{4,12},{8,0},{12,4},{16,24},{20,28},{24,16},{28,20},{1,9},{5... | collective-permute-start | bytes 3145736 | tf_op jit(solution)/shard_map/ppermute | solution.py:295
  528.9 39.8 %collective-permute-start.52 = (bf16[512,1024]{1,0:T(8,128)(2,1)S(1)}, bf16[512,1024]{1,0:T(8,128)(2,1)}, u32[]{:S(2)}, u32[]{:S(2)}) collective-permute-start(bf16[512,1024]{1,0:T(8,128)(2,1)S(1)} %pad_maximum_fusion.3.refs_0_), channel_id=1, source_target_pairs={{0,4},{4,0},{8,12},{12,8},{16,20},{20,16},{24,28},{28,24},{1,5},{5... | collective-permute-start | bytes 3145736 | tf_op jit(solution)/shard_map/ppermute | solution.py:295
  529.0 28.8 %collective-permute-start.7 = (bf16[256,768]{1,0:T(8,128)(2,1)}, bf16[256,768]{1,0:T(8,128)(2,1)}, u32[]{:S(2)}, u32[]{:S(2)}) collective-permute-start(bf16[256,768]{1,0:T(8,128)(2,1)} %add_convert_fusion.18), channel_id=1, source_target_pairs={{0,16},{4,20},{8,24},{12,28},{16,0},{20,4},{24,8},{28,12},{1,17},{... | collective-permute-start | bytes 1179656 | tf_op jit(solution)/shard_map/ppermute | solution.py:295
  563.6 28.6 %collective-permute-start.57 = (bf16[512,1024]{1,0:T(8,128)(2,1)}, bf16[512,1024]{1,0:T(8,128)(2,1)}, u32[]{:S(2)}, u32[]{:S(2)}) collective-permute-start(bf16[512,1024]{1,0:T(8,128)(2,1)} %pad_maximum_fusion.4.refs_4_), channel_id=1, source_target_pairs={{0,16},{4,20},{8,24},{12,28},{16,0},{20,4},{24,8},{28,12},{1,17},{... | collective-permute-start | bytes 3145736 | tf_op jit(solution)/shard_map/ppermute | solution.py:295
  567.3 25.8 %collective-permute-start.58 = (bf16[512,1024]{1,0:T(8,128)(2,1)}, bf16[512,1024]{1,0:T(8,128)(2,1)}, u32[]{:S(2)}, u32[]{:S(2)}) collective-permute-start(bf16[512,1024]{1,0:T(8,128)(2,1)} %pad_maximum_fusion.4.refs_4_), channel_id=1, source_target_pairs={{0,4},{4,0},{8,12},{12,8},{16,20},{20,16},{24,28},{28,24},{1,5},{5... | collective-permute-start | bytes 3145736 | tf_op jit(solution)/shard_map/ppermute | solution.py:295
  568.3 30.5 %collective-permute-start.40 = (bf16[512,1024]{1,0:T(8,128)(2,1)}, bf16[512,1024]{1,0:T(8,128)(2,1)}, u32[]{:S(2)}, u32[]{:S(2)}) collective-permute-start(bf16[512,1024]{1,0:T(8,128)(2,1)} %collective-permute-done.38.refs_1_), channel_id=1, source_target_pairs={{0,4},{4,0},{8,12},{12,8},{16,20},{20,16},{24,28},{28,24},{1,5},{5... | collective-permute-start | bytes 3145736 | tf_op jit(solution)/shard_map/ppermute | solution.py:295
  568.8 30.1 %collective-permute-start.46 = (bf16[512,1024]{1,0:T(8,128)(2,1)}, bf16[512,1024]{1,0:T(8,128)(2,1)}, u32[]{:S(2)}, u32[]{:S(2)}) collective-permute-start(bf16[512,1024]{1,0:T(8,128)(2,1)} %collective-permute-done.44.refs_5_), channel_id=1, source_target_pairs={{0,4},{4,0},{8,12},{12,8},{16,20},{20,16},{24,28},{28,24},{1,5},{5... | collective-permute-start | bytes 3145736 | tf_op jit(solution)/shard_map/ppermute | solution.py:295
  581.4 23.3 %collective-permute-start.53 = (bf16[512,1024]{1,0:T(8,128)(2,1)}, bf16[512,1024]{1,0:T(8,128)(2,1)}, u32[]{:S(2)}, u32[]{:S(2)}) collective-permute-start(bf16[512,1024]{1,0:T(8,128)(2,1)} %collective-permute-done.51.refs_1_), channel_id=1, source_target_pairs={{0,4},{4,0},{8,12},{12,8},{16,20},{20,16},{24,28},{28,24},{1,5},{5... | collective-permute-start | bytes 3145736 | tf_op jit(solution)/shard_map/ppermute | solution.py:295
  592.2 17.3 %collective-permute-start.9 = (bf16[512,768]{1,0:T(8,128)(2,1)}, bf16[512,768]{1,0:T(8,128)(2,1)}, u32[]{:S(2)}, u32[]{:S(2)}) collective-permute-start(bf16[512,768]{1,0:T(8,128)(2,1)} %pad_maximum_fusion.5.refs_0_), channel_id=1, source_target_pairs={{0,8},{4,12},{8,0},{12,4},{16,24},{20,28},{24,16},{28,20},{1,9},{5... | collective-permute-start | bytes 2359304 | tf_op jit(solution)/shard_map/ppermute | solution.py:295
  593.1 17.3 %collective-permute-start.15 = (bf16[512,768]{1,0:T(8,128)(2,1)}, bf16[512,768]{1,0:T(8,128)(2,1)}, u32[]{:S(2)}, u32[]{:S(2)}) collective-permute-start(bf16[512,768]{1,0:T(8,128)(2,1)} %pad_maximum_fusion.6.refs_4_), channel_id=1, source_target_pairs={{0,16},{4,20},{8,24},{12,28},{16,0},{20,4},{24,8},{28,12},{1,17},{... | collective-permute-start | bytes 2359304 | tf_op jit(solution)/shard_map/ppermute | solution.py:295
  610.4 50.7 %collective-permute-start.16 = (bf16[512,768]{1,0:T(8,128)(2,1)}, bf16[512,768]{1,0:T(8,128)(2,1)}, u32[]{:S(2)}, u32[]{:S(2)}) collective-permute-start(bf16[512,768]{1,0:T(8,128)(2,1)} %pad_maximum_fusion.6.refs_4_), channel_id=1, source_target_pairs={{0,4},{4,0},{8,12},{12,8},{16,20},{20,16},{24,28},{28,24},{1,5},{5... | collective-permute-start | bytes 2359304 | tf_op jit(solution)/shard_map/ppermute | solution.py:295
  610.4 50.7 %collective-permute-start.11 = (bf16[512,768]{1,0:T(8,128)(2,1)}, bf16[512,768]{1,0:T(8,128)(2,1)}, u32[]{:S(2)}, u32[]{:S(2)}) collective-permute-start(bf16[512,768]{1,0:T(8,128)(2,1)} %collective-permute-done.9.refs_1_), channel_id=1, source_target_pairs={{0,4},{4,0},{8,12},{12,8},{16,20},{20,16},{24,28},{28,24},{1,5},{5... | collective-permute-start | bytes 2359304 | tf_op jit(solution)/shard_map/ppermute | solution.py:295
  613.2 47.9 %collective-permute-start.17 = (bf16[512,768]{1,0:T(8,128)(2,1)}, bf16[512,768]{1,0:T(8,128)(2,1)}, u32[]{:S(2)}, u32[]{:S(2)}) collective-permute-start(bf16[512,768]{1,0:T(8,128)(2,1)} %collective-permute-done.15.refs_5_), channel_id=1, source_target_pairs={{0,4},{4,0},{8,12},{12,8},{16,20},{20,16},{24,28},{28,24},{1,5},{5... | collective-permute-start | bytes 2359304 | tf_op jit(solution)/shard_map/ppermute | solution.py:295
  613.2 78.0 %collective-permute-start.32 = (f32[2562]{0:T(1024)S(1)}, f32[2562]{0:T(1024)S(1)}, u32[]{:S(2)}, u32[]{:S(2)}) collective-permute-start(f32[2562]{0:T(1024)S(1)} %add.256), channel_id=1, source_target_pairs={{0,8},{4,12},{8,0},{12,4},{16,24},{20,28},{24,16},{28,20},{1,9},{5... | collective-permute-start | bytes 30752 | tf_op jit(solution)/shard_map/ppermute | solution.py:295
  615.1 76.4 %collective-permute-start.4 = (f32[2560]{0:T(1024)S(1)}, f32[2560]{0:T(1024)S(1)}, u32[]{:S(2)}, u32[]{:S(2)}) collective-permute-start(f32[2560]{0:T(1024)S(1)} %add.242), channel_id=1, source_target_pairs={{0,16},{4,20},{8,24},{12,28},{16,0},{20,4},{24,8},{28,12},{1,17},{... | collective-permute-start | bytes 30728 | tf_op jit(solution)/shard_map/ppermute | solution.py:295
  (88 other events, 975.5 us)
Sparse Core Ops, SparseCore 0:
  10.2 66.1 all-gather.2
  78.5 62.0 all-gather.4
  279.4 58.3 reduce-scatter.4
  340.0 60.3 reduce-scatter.2

commit v2 on v1

--- a/solution.py
+++ b/solution.py
@@ -4,6 +4,7 @@
 import jax.numpy as jnp
 from jax import lax
 from jax.experimental import pallas as pl
+from jax.experimental.layout import Layout, with_layout_constraint
 from jax.experimental.pallas import tpu as pltpu
 from jax.sharding import PartitionSpec as P
 
@@ -12,7 +13,6 @@
 HALF = ROT // 2
 BLK = 128
 TILE = 512
-LANES = 128
 
 epsilon = 1e-05
 masked_score = -1e30
@@ -20,6 +20,10 @@
 log2e = 1.4426950408889634
 f32 = jnp.float32
 bf16 = jnp.bfloat16
+
+
+def row_major(value):
+    return with_layout_constraint(value, Layout(tuple(range(value.ndim))))
 
 
 def token_table(seq_lengths, padding, initial):
@@ -312,69 +316,109 @@
     return [s | bits[0] for s in rest] + rest
 
 
-def product_kernel(lhs_dim, rhs_dim, cuts, with_add, order_ref, lhs_ref, rhs_ref, *refs):
+def product_kernel(dims, tiles, orders, table_ref, *refs):
     step = pl.program_id(0)
-    piece = lax.dot_general(
-        lhs_ref[...], rhs_ref[...], (((lhs_dim,), (rhs_dim,)), ((), ())), preferred_element_type=f32
-    )
-    if with_add:
-        piece = piece + refs[0][...].astype(f32)
-    piece = piece.astype(bf16)
-    outs = refs[1:] if with_add else refs
-    for out, first, count in zip(outs, cuts, cuts[1:] + [None]):
-        if len(outs) == 1:
-            out[...] = piece
+    count = len(orders[0])
+    pieces = [refs[k * (count + 1) : k * (count + 1) + count] for k in range(len(dims))]
+    factors = [refs[k * (count + 1) + count] for k in range(len(dims))]
+    refs = refs[len(dims) * (count + 1) :]
+    refs, stacks = refs[: -len(dims)], refs[-len(dims) :]
+
+    @pl.when(step == 0)
+    def _():
+        for stack, parts, (lhs_dim, unused) in zip(stacks, pieces, dims):
+            rows = parts[0].shape[1 - lhs_dim]
+            for p, part in enumerate(parts):
+                if lhs_dim == 0:
+                    stack[:, p * rows : (p + 1) * rows] = part[...]
+                else:
+                    stack[p * rows : (p + 1) * rows, :] = part[...]
+
+    at = 0
+    for stack, factor, (lhs_dim, rhs_dim) in zip(stacks, factors, dims):
+        product = lax.dot_general(
+            stack[...],
+            factor[...],
+            (((lhs_dim,), (rhs_dim,)), ((), ())),
+            preferred_element_type=f32,
+        )
+        columns = slice(at, at + product.shape[1])
+        at += product.shape[1]
+        if len(refs) == 1:
+            refs[0][:, columns] = product.astype(bf16)
+            continue
+        added, outs = refs[0], refs[1:]
+        product = (product + added[:, columns].astype(f32)).astype(bf16)
+        rows = product.shape[0] // count
+        for half, order in enumerate(orders):
+
+            @pl.when(step // tiles == half)
+            def _(half=half, order=order, product=product, columns=columns, rows=rows):
+                for p, slot in enumerate(order):
+                    source = orders[0].index(slot)
+                    out = outs[2 * half + p // (count // 2)]
+                    first = p % (count // 2) * rows
+                    out[first : first + rows, columns] = product[
+                        source * rows : (source + 1) * rows
+                    ]
+
+
+def piece_products(owners, size, pairs, orders, added):
+    count = len(orders[0])
+    tiles = 2 if len(pairs) == 1 else 1
+    in_specs, operands, scratch, width, flops = [], [], [], 0, 0
+    for lhs, rhs, lhs_dim, rhs_dim in pairs:
+        tokens = lhs.shape[lhs_dim]
+        rows = lhs.shape[1 - lhs_dim] // size
+        columns = rhs.shape[1 - rhs_dim] // (2 * tiles)
+        width += columns
+        flops += 4 * tiles * count * rows * columns * tokens
+        for p in range(count):
+            if lhs_dim == 0:
+                in_specs.append(pl.BlockSpec((tokens, rows), lambda i, t, p=p: (0, t[p])))
+            else:
+                in_specs.append(pl.BlockSpec((rows, tokens), lambda i, t, p=p: (t[p], 0)))
+            operands.append(lhs)
+        if rhs_dim == 0:
+            in_specs.append(pl.BlockSpec((tokens, columns), lambda i, t: (0, i)))
         else:
-            inside = step >= first if count is None else (step >= first) & (step < count)
-
-            @pl.when(inside)
-            def _(out=out):
-                out[...] = piece
-
-
-def piece_products(owners, lhs, rhs, lhs_dim, rhs_dim, columns, half, added, cuts):
-    steps = owners[0].shape[0]
-    size = owners[1]
-    rows = lhs.shape[1 - lhs_dim] // size
-    tokens = lhs.shape[lhs_dim]
-    table = owners[0].astype(jnp.int32)
-    if added is not None:
-        table = jnp.concatenate([table, jnp.array(added[1], jnp.int32)])
-    lhs_block = (tokens, rows) if lhs_dim == 0 else (rows, tokens)
-    rhs_block = (tokens, columns) if rhs_dim == 0 else (columns, tokens)
-    in_specs = [
-        pl.BlockSpec(lhs_block, (lambda i, t: (0, t[i])) if lhs_dim == 0 else (lambda i, t: (t[i], 0))),
-        pl.BlockSpec(rhs_block, (lambda i, t: (0, half)) if rhs_dim == 0 else (lambda i, t: (half, 0))),
-    ]
-    operands = [lhs, rhs]
-    if added is not None:
-        in_specs.append(pl.BlockSpec((rows, columns), lambda i, t: (t[steps + i], half)))
-        operands.append(added[0])
-    ends = cuts[1:] + [steps]
-    out_specs = [
-        pl.BlockSpec(
-            (rows, columns),
-            lambda i, t, first=first, last=end - 1: (jnp.clip(i, first, last) - first, 0),
-        )
-        for first, end in zip(cuts, ends)
-    ]
+            in_specs.append(pl.BlockSpec((columns, tokens), lambda i, t: (i, 0)))
+        operands.append(rhs)
+        stack = (tokens, count * rows) if lhs_dim == 0 else (count * rows, tokens)
+        scratch.append(pltpu.VMEM(stack, bf16))
+    if added is None:
+        out_shape = [jax.ShapeDtypeStruct((count * rows, 2 * tiles * width), bf16)]
+        out_specs = [pl.BlockSpec((count * rows, width), lambda i, t: (0, i))]
+    else:
+        in_specs.append(pl.BlockSpec((count * rows, width), lambda i, t: (0, i)))
+        operands.append(added)
+        out_shape = [jax.ShapeDtypeStruct((count // 2 * rows, tiles * width), bf16)] * 4
+        out_specs = [
+            pl.BlockSpec(
+                (count // 2 * rows, width),
+                lambda i, t, at=half * tiles: (0, jnp.clip(i - at, 0, tiles - 1)),
+            )
+            for half in (0, 0, 1, 1)
+        ]
+    dims = [(lhs_dim, rhs_dim) for unused, unused_too, lhs_dim, rhs_dim in pairs]
     return pl.pallas_call(
-        functools.partial(product_kernel, lhs_dim, rhs_dim, cuts, added is not None),
+        functools.partial(product_kernel, dims, tiles, orders),
         name="piece_products",
-        out_shape=[
-            jax.ShapeDtypeStruct((rows * (end - first), columns), bf16)
-            for first, end in zip(cuts, ends)
-        ],
+        out_shape=out_shape,
         grid_spec=pltpu.PrefetchScalarGridSpec(
-            num_scalar_prefetch=1, grid=(steps,), in_specs=in_specs, out_specs=out_specs
-        ),
-        compiler_params=pltpu.CompilerParams(vmem_limit_bytes=48 * 2**20),
+            num_scalar_prefetch=1,
+            grid=(2 * tiles,),
+            in_specs=in_specs,
+            out_specs=out_specs,
+            scratch_shapes=scratch,
+        ),
+        compiler_params=pltpu.CompilerParams(vmem_limit_bytes=52 * 2**20),
         cost_estimate=pl.CostEstimate(
-            flops=2 * steps * rows * columns * tokens,
-            bytes_accessed=2 * (steps * rows * (tokens + columns * 2) + columns * tokens),
+            flops=flops,
+            bytes_accessed=4 * tiles * width * (2 * count * rows + tokens),
             transcendentals=0,
         ),
-    )(table, *operands)
+    )(owners.astype(jnp.int32), *operands)
 
 
 def halves_orders(size):
@@ -382,90 +426,156 @@
     return [(upper, slot_order(upper)), (upper[::-1], slot_order(upper[::-1]))]
 
 
-def piece_sums(index, size, lhs, rhs, lhs_dim, rhs_dim):
-    orders = halves_orders(size)
-    columns = rhs.shape[1 - rhs_dim]
-    if lhs_dim == 0 and (lhs.shape[1] // size) % LANES:
-        lhs, lhs_dim = jnp.transpose(lhs), 1
-    first_order = orders[0][1]
-    far = index ^ jnp.array([s | 1 for s in first_order], jnp.int32)
-    sent = piece_products((far, size), lhs, rhs, lhs_dim, rhs_dim, columns, 0, None, [0])[0]
-    got = swap(sent, "dp", size, 1)
-    pieces = []
-    for half, (bits, order) in enumerate(orders):
-        near = index ^ jnp.array(order, jnp.int32)
-        rows_at = [first_order.index(s) for s in order]
-        send, keep = piece_products(
-            (near, size), lhs, rhs, lhs_dim, rhs_dim, columns // 2, half, (got, rows_at),
-            [0, size // 4],
-        )
-        for bit in bits:
-            got_piece = swap(send, "dp", size, bit)
-            cut = keep.shape[0] // 2
-            if bit == bits[-1]:
-                keep = (keep.astype(f32) + got_piece.astype(f32)).astype(bf16)
-            else:
-                send = (keep[:cut].astype(f32) + got_piece[:cut].astype(f32)).astype(bf16)
-                keep = (keep[cut:].astype(f32) + got_piece[cut:].astype(f32)).astype(bf16)
-        pieces.append(keep)
-    return pieces
-
-
-def spread_kernel(quarter, parts, table_ref, *refs):
-    ins, out = refs[:-1], refs[-1]
+def tie(*values):
+    return lax.optimization_barrier(values)
+
+
+class PieceSum:
+    def __init__(self, index, size, *pairs):
+        self.index, self.size = index, size
+        self.orders = halves_orders(size)
+        self.bits = [bits for bits, unused in self.orders]
+        self.pairs = pairs
+        self.spreading = self.finished = False
+
+    def swaps(self, values):
+        bits = [half[self.level] for half in self.bits]
+        self.pending = [swap(v, "dp", self.size, bit) for v, bit in zip(values, bits)]
+
+    def across_cores(self):
+        far = self.index ^ jnp.array([s | 1 for s in self.orders[0][1]], jnp.int32)
+        orders = [order for unused, order in self.orders]
+        self.kept = piece_products(far, self.size, self.pairs, orders, None)
+        self.pending = [swap(self.kept[0], "dp", self.size, 1)]
+
+    def products(self):
+        near = self.index ^ jnp.array(self.orders[0][1], jnp.int32)
+        orders = [order for unused, order in self.orders]
+        made = piece_products(near, self.size, self.pairs, orders, self.pending[0])
+        sends, self.kept = [made[0], made[2]], [made[1], made[3]]
+        self.level = 0
+        self.swaps(sends)
+
+    def advance(self):
+        if self.spreading:
+            self.advance_spread()
+            return
+        self.level += 1
+        if self.level < len(self.bits[0]):
+            sends, keeps = [], []
+            for keep, got in zip(self.kept, self.pending):
+                cut = keep.shape[0] // 2
+                sends.append((keep[:cut].astype(f32) + got[:cut].astype(f32)).astype(bf16))
+                keeps.append((keep[cut:].astype(f32) + got[cut:].astype(f32)).astype(bf16))
+            self.kept = keeps
+            self.swaps(sends)
+            return
+        self.kept = [
+            (keep.astype(f32) + got.astype(f32)).astype(bf16)
+            for keep, got in zip(self.kept, self.pending)
+        ]
+        self.slots = [[0], [0]]
+        self.spreading = True
+        self.level -= 1
+        self.swaps(self.kept)
+
+    def advance_spread(self):
+        if self.level > 0:
+            self.kept = [jnp.concatenate(p, axis=0) for p in zip(self.kept, self.pending)]
+            self.slots = [
+                have + [s | half[self.level] for s in have]
+                for have, half in zip(self.slots, self.bits)
+            ]
+            self.level -= 1
+            self.swaps(self.kept)
+        elif self.level == 0:
+            self.others = self.pending
+            self.level = -1
+            self.pending = [swap(v, "dp", self.size, 1) for v in self.kept + self.others]
+        else:
+            self.finished = True
+
+    def spread(self, *layout):
+        while not self.finished:
+            arrived([self])
+            self.advance()
+        arrays, slots = [], []
+        for h in range(2):
+            have = self.slots[h]
+            other = [s | self.bits[h][0] for s in have]
+            arrays += [self.kept[h], self.others[h], self.pending[h], self.pending[h + 2]]
+            slots += have + other + [s | 1 for s in have + other]
+        return spread(self.index, self.size, arrays, slots, layout)
+
+
+def arrived(sums, *values):
+    count = [len(s.pending) for s in sums]
+    out = list(tie(*[p for s in sums for p in s.pending], *values))
+    for s, n in zip(sums, count):
+        s.pending, out = out[:n], out[n:]
+    return out
+
+
+def computed(sums, *values):
+    count = [len(s.kept) for s in sums]
+    out = list(tie(*[p for s in sums for p in s.kept], *values))
+    for s, n in zip(sums, count):
+        s.kept, out = out[:n], out[n:]
+    return out
+
+
+def spread_kernel(quarter, layout, table_ref, *refs):
+    ins, outs = refs[:8], refs[8:]
     step = pl.program_id(0)
     for j, piece in enumerate(ins):
 
         @pl.when(step // quarter == j)
         def _(piece=piece):
-            if parts == 1:
-                out[...] = piece[...].astype(f32)
-            else:
-                wide = piece.shape[1] // parts
+            at = 0
+            for out, (parts, columns, transposed) in zip(outs, layout):
                 for c in range(parts):
-                    out[:, c, :] = piece[:, c * wide : (c + 1) * wide].astype(f32)
-
-
-def spread(index, size, pieces, parts):
-    arrays, slots = [], []
-    for (bits, unused), piece in zip(halves_orders(size), pieces):
-        have, have_slots = piece, [0]
-        for bit in bits[:0:-1]:
-            have = jnp.concatenate([have, swap(have, "dp", size, bit)], axis=0)
-            have_slots = have_slots + [s | bit for s in have_slots]
-        other = swap(have, "dp", size, bits[0])
-        other_slots = [s | bits[0] for s in have_slots]
-        arrays += [have, other, swap(have, "dp", size, 1), swap(other, "dp", size, 1)]
-        slots += have_slots + other_slots
-        slots += [s | 1 for s in have_slots] + [s | 1 for s in other_slots]
+                    block = piece[:, at : at + columns].astype(f32)
+                    at += columns
+                    if parts > 1:
+                        out[c] = block
+                    else:
+                        out[...] = jnp.transpose(block) if transposed else block
+
+
+def spread(index, size, arrays, slots, layout):
     table = index ^ jnp.array(slots, jnp.int32)
     quarter = size // 4
-    rows, columns = pieces[0].shape
+    rows, width = arrays[0].shape[0] // quarter, arrays[0].shape[1]
     in_specs = [
         pl.BlockSpec(
-            (rows, columns),
+            (rows, width),
             lambda i, t, at=j * quarter: (jnp.clip(i - at, 0, quarter - 1), 0),
         )
         for j in range(8)
     ]
-    if parts == 1:
-        out_shape = (rows * size, 2 * columns)
-        out_spec = pl.BlockSpec((rows, columns), lambda i, t: (t[i], i // size))
-    else:
-        out_shape = (rows * size, parts, 2 * columns // parts)
-        out_spec = pl.BlockSpec(
-            (rows, parts, columns // parts), lambda i, t: (t[i], 0, i // size)
-        )
+    out_shape, out_specs = [], []
+    for parts, columns, transposed in layout:
+        if parts > 1:
+            out_shape.append((parts, rows * size, 2 * columns))
+            out_specs.append(
+                pl.BlockSpec((parts, rows, columns), lambda i, t: (0, t[i], i // size))
+            )
+        elif transposed:
+            out_shape.append((2 * columns, rows * size))
+            out_specs.append(pl.BlockSpec((columns, rows), lambda i, t: (i // size, t[i])))
+        else:
+            out_shape.append((rows * size, 2 * columns))
+            out_specs.append(pl.BlockSpec((rows, columns), lambda i, t: (t[i], i // size)))
     return pl.pallas_call(
-        functools.partial(spread_kernel, quarter, parts),
+        functools.partial(spread_kernel, quarter, layout),
         name="spread",
-        out_shape=jax.ShapeDtypeStruct(out_shape, f32),
+        out_shape=[jax.ShapeDtypeStruct(shape, f32) for shape in out_shape],
         grid_spec=pltpu.PrefetchScalarGridSpec(
-            num_scalar_prefetch=1, grid=(2 * size,), in_specs=in_specs, out_specs=out_spec
+            num_scalar_prefetch=1, grid=(2 * size,), in_specs=in_specs, out_specs=out_specs
         ),
         compiler_params=pltpu.CompilerParams(vmem_limit_bytes=48 * 2**20),
         cost_estimate=pl.CostEstimate(
-            flops=0, bytes_accessed=rows * columns * size * 12, transcendentals=0
+            flops=0, bytes_accessed=rows * width * size * 12, transcendentals=0
         ),
     )(table, *arrays)
 
@@ -516,8 +626,13 @@
             got = jnp.sum(got, axis=0).astype(bf16)
         return got
 
-    full_in = lax.all_gather(hidden_in.astype(bf16), "tensor", axis=1, tiled=True).astype(f32)
+    full_in = lax.all_gather(hidden_in.astype(bf16), "tensor", axis=1, tiled=True)
     grad_proj = lax.all_gather(cotangent.astype(bf16), "tensor", axis=1, tiled=True)
+    w_back = row_major(jnp.transpose(w_qkv, (1, 2, 0)))
+    full_in, w_back, cosine, sine, cosine_all, sine_all, place, seq = tie(
+        full_in, w_back, cosine, sine, cosine_all, sine_all, place, seq
+    )
+    full_in = full_in.astype(f32)
     row_mean = jnp.mean(full_in, axis=-1, keepdims=True)
     centered = full_in - row_mean
     inv_std = lax.rsqrt(jnp.mean(centered * centered, axis=-1, keepdims=True) + epsilon)
@@ -538,17 +653,66 @@
     )
     packed = jnp.concatenate([rotated[0], rotated[1], projections[2]], axis=1).astype(bf16)
     parts = to_heads(packed)
-    out_stack, lse, seq_out = attention_forward(place, seq, rank, parts, split)
-    attended = to_tokens(out_stack).reshape(heads * HD, tok_local)
-
     hidden_pre = jnp.dot(normed, w_fc1, preferred_element_type=f32) + b_fc1
     activated = gelu_tanh(hidden_pre).astype(bf16)
+    activated_t, normed_t = row_major(jnp.transpose(activated)), row_major(jnp.transpose(normed))
+    parts, hidden_pre, activated, activated_t, normed_t, grad_proj = tie(
+        parts, hidden_pre, activated, activated_t, normed_t, grad_proj
+    )
+
+    def new_sum(*pairs):
+        made = PieceSum(data_index, dp_size, *pairs)
+        made.across_cores()
+        return made
+
+    sum_fc2 = new_sum((activated_t, grad_proj, 1, 0))
+    (grad_proj,) = computed([sum_fc2], grad_proj)
+    grad_attended = jnp.einsum(
+        "ed,td->et", w_dense, grad_proj, preferred_element_type=f32
+    ).astype(bf16)
+    (grad_attended,) = arrived([sum_fc2], grad_attended)
+    grad_stack = to_heads(grad_attended.reshape(heads, HD, tok_local))
+    sum_fc2.products()
+    grad_proj, hidden_pre = computed([sum_fc2], grad_proj, hidden_pre)
+    grad_act = jnp.einsum("td,fd->tf", grad_proj, w_fc2, preferred_element_type=f32)
+    unused_value, gelu_back = jax.vjp(gelu_tanh, hidden_pre)
+    grad_hidden = gelu_back(grad_act)[0].astype(bf16)
+    (grad_hidden,) = arrived([sum_fc2], grad_hidden)
+    sum_fc1 = new_sum((normed_t, grad_hidden, 1, 0))
+    sum_fc1.kept = arrived([sum_fc1], *sum_fc1.kept)
+    sum_fc2.advance()
+    sum_fc1.pending = computed([sum_fc2], *sum_fc1.pending)
+    sum_fc1.products()
+
+    (parts,) = computed([sum_fc2, sum_fc1], parts)
+    out_stack, lse, seq_out = attention_forward(place, seq, rank, parts, split)
+    out_stack, grad_stack, lse = arrived([sum_fc2, sum_fc1], out_stack, grad_stack, lse)
+    attended = to_tokens(out_stack).reshape(heads * HD, tok_local)
+    sum_fc2.advance()
+    sum_fc1.advance()
+    (lse,) = computed([sum_fc2, sum_fc1], lse)
+    grad_pieces = attention_backward(
+        place, seq, rank, parts, grad_stack, lse, seq_out, cosine_all, sine_all, split
+    )
+    grad_pieces, attended, grad_hidden, activated = arrived(
+        [sum_fc2, sum_fc1], grad_pieces, attended, grad_hidden, activated
+    )
+
+    grad_qkv = to_tokens(grad_pieces).reshape(heads, 3, HD, tok_local)
     partial_value = jnp.einsum(
         "et,ed->td", attended, w_dense, preferred_element_type=f32
     ) + jnp.dot(activated, w_fc2, preferred_element_type=f32)
+    partial_value = partial_value.astype(bf16)
     projected = lax.psum_scatter(
-        partial_value.astype(bf16), "tensor", scatter_dimension=1, tiled=True
+        partial_value, "tensor", scatter_dimension=1, tiled=True
     ).astype(f32)
+    grad_normed = jnp.einsum("tf,df->td", grad_hidden, w_fc1, preferred_element_type=f32)
+    grad_qkv, grad_normed, partial_value, *waiting = tie(
+        grad_qkv, grad_normed, partial_value, *sum_fc2.pending, *sum_fc1.pending
+    )
+    sum_fc2.pending, sum_fc1.pending = waiting[:2], waiting[2:]
+    sum_fc2.advance()
+    sum_fc1.advance()
     branch = projected + b_dense + b_fc2
     output = hidden_in + branch
     valid_rows = my_valid.astype(f32)[:, None]
@@ -556,51 +720,46 @@
     sum_branch = jnp.sum(branch * branch * valid_rows)
     valid_count = jnp.sum(valid_all.astype(f32)) * model_width
 
-    grad_attended = jnp.einsum(
-        "ed,td->et", w_dense, grad_proj, preferred_element_type=f32
-    ).astype(bf16)
-    grad_stack = to_heads(grad_attended.reshape(heads, HD, tok_local))
-    grad_act = jnp.einsum("td,fd->tf", grad_proj, w_fc2, preferred_element_type=f32)
-    unused_value, gelu_back = jax.vjp(gelu_tanh, hidden_pre)
-    grad_hidden = gelu_back(grad_act)[0].astype(bf16)
     grad_b_fc1 = jnp.sum(grad_hidden.astype(f32), axis=0)
-    grad_normed = jnp.einsum("tf,df->td", grad_hidden, w_fc1, preferred_element_type=f32)
-
-    def weight_sum(lhs, rhs, lhs_dim, rhs_dim, parts_out):
-        pieces = piece_sums(data_index, dp_size, lhs, rhs, lhs_dim, rhs_dim)
-        return spread(data_index, dp_size, pieces, parts_out)
-
-    grad_w_fc2 = weight_sum(activated, grad_proj, 0, 0, 1)
-    grad_w_fc1 = weight_sum(normed, grad_hidden, 0, 0, 1)
-    grad_w_dense = weight_sum(attended, grad_proj, 1, 0, 1)
-
-    early = jnp.concatenate(
-        [jnp.sum(cotangent, axis=0), grad_b_fc1, sum_output[None], sum_branch[None]]
-    )
-    early = all_sum(early, "dp", dp_size)
-    totals = all_sum(early[-2:], "tensor", model_width // dim_local)
-
-    grad_pieces = attention_backward(
-        place, seq, rank, parts, grad_stack, lse, seq_out, cosine_all, sine_all, split
-    )
-    grad_qkv = to_tokens(grad_pieces).reshape(heads, 3, HD, tok_local)
     grad_b_qkv = jnp.transpose(jnp.sum(grad_qkv.astype(f32), axis=3), (1, 0, 2))
     by_half = jnp.transpose(
         grad_qkv.reshape(2, heads // 2, 3, HD, tok_local), (0, 2, 1, 3, 4)
     ).reshape(3 * heads * HD, tok_local)
-    grad_w_qkv = weight_sum(normed, by_half, 0, 1, 3)
-    grad_normed = grad_normed + jnp.einsum(
-        "hcet,dche->td",
-        grad_qkv,
-        w_qkv.reshape(model_width, 3, heads, HD),
-        preferred_element_type=f32,
-    )
+    sum_qkv = new_sum((normed_t, by_half, 1, 1), (grad_proj, attended, 0, 1))
+    (grad_qkv,) = computed([sum_qkv], grad_qkv)
+    grad_normed = row_major(
+        grad_normed
+        + jnp.einsum(
+            "hcet,ched->td",
+            grad_qkv,
+            w_back.reshape(3, heads, HD, model_width),
+            preferred_element_type=f32,
+        )
+    )
+    grad_narrow = grad_normed.astype(bf16)
+    (grad_narrow,) = arrived([sum_qkv, sum_fc2], grad_narrow)
     grad_local = lax.psum_scatter(
-        grad_normed.astype(bf16), "tensor", scatter_dimension=1, tiled=True
+        grad_narrow, "tensor", scatter_dimension=1, tiled=True
     ).astype(f32)
+    sum_qkv.products()
+    sum_qkv.kept = arrived([sum_fc1], *sum_qkv.kept)
+    sum_fc2.advance()
+    sum_fc1.advance()
+    sum_fc2.pending = computed([sum_qkv], *sum_fc2.pending)
+    (grad_w_fc2,) = sum_fc2.spread((1, model_width // 2, False))
+    (grad_w_fc2,) = arrived([sum_fc1, sum_qkv], grad_w_fc2)
+    sum_fc1.advance()
+    sum_qkv.advance()
     scaled = grad_normed * gain
     mean_sums = jnp.stack([jnp.sum(scaled, axis=1), jnp.sum(scaled * normal_x, axis=1)])
-    mean_sums = all_sum(mean_sums, "tensor", model_width // dim_local) / model_width
+    shared = jnp.concatenate([mean_sums.reshape(-1), sum_output[None], sum_branch[None]])
+    sum_fc1.pending = computed([sum_qkv], *sum_fc1.pending)
+    sum_fc1.advance()
+    (grad_w_fc1,) = sum_fc1.spread((1, w_fc1.shape[1] // 2, False))
+    grad_w_fc1, shared = arrived([sum_qkv], grad_w_fc1, shared)
+    sum_qkv.advance()
+    shared = all_sum(shared, "tensor", model_width // dim_local)
+    mean_sums = shared[:-2].reshape(2, tok_local) / model_width
     mean_one, mean_two = mean_sums[0][:, None], mean_sums[1][:, None]
     gain_local = lax.dynamic_slice_in_dim(gain, tensor_index * dim_local, dim_local)
     normal_local = lax.dynamic_slice_in_dim(normal_x, tensor_index * dim_local, dim_local, 1)
@@ -611,23 +770,36 @@
         [
             jnp.sum(grad_local * normal_local, axis=0),
             jnp.sum(grad_local, axis=0),
+            jnp.sum(cotangent, axis=0),
+            grad_b_fc1,
             grad_b_qkv.reshape(-1),
+            shared[-2:],
         ]
     )
+    cuts = [dim_local, 2 * dim_local, 3 * dim_local, 3 * dim_local + grad_b_fc1.shape[0]]
     late = all_sum(late, "dp", dp_size)
+    while not sum_qkv.finished:
+        arrived([sum_qkv])
+        sum_qkv.advance()
+    sum_qkv.pending[0], late = tie(sum_qkv.pending[0], late)
+    grad_w_qkv, grad_w_dense = sum_qkv.spread(
+        (3, heads * HD // 2, False), (1, heads * HD // 2, True)
+    )
+    grad_w_qkv = jnp.transpose(grad_w_qkv, (1, 0, 2))
+    totals = late[-2:]
     rms = jnp.sqrt(totals / valid_count)
-    bias_grad = early[:dim_local]
+    bias_grad = late[cuts[1] : cuts[2]]
     return (
         output,
         grad_input,
-        late[:dim_local],
-        late[dim_local : 2 * dim_local],
+        late[: cuts[0]],
+        late[cuts[0] : cuts[1]],
         grad_w_qkv,
-        late[2 * dim_local :].reshape(3, heads * HD),
+        late[cuts[3] : -2].reshape(3, heads * HD),
         grad_w_dense,
         bias_grad,
         grad_w_fc1,
-        early[dim_local:-2],
+        late[cuts[2] : cuts[3]],
         grad_w_fc2,
         bias_grad,
         rms[0],

time: 724 us -> 586 us (0.81)
  waiting for transfers between devices: 269 us -> 163 us
  Pallas kernels: 190 us -> 173 us
  starting transfers between devices: 61.3 us -> 48.9 us
  other arithmetic: 48.4 us -> 56.7 us
    ppermute x62 -> x44, waiting for transfers between devices: 171 us -> 101 us  [swap(): return lax.ppermute(value, axis, [(i, i ^ offset) for i in range(size)])]
    all_gather x1, waiting for transfers between devices: 43.5 us -> 8.08 us  [local(): lax.all_gather(cotangent.astype(bf16), 'tensor', axis=1, tiled=True)]
    unnamed x135 -> x111, local copies, waits for them, and re-layouts: 42.3 us -> 18.2 us
    pallas_call x16 -> x9, Pallas kernels: 119 us -> 96.8 us  [the longest x6 53.9 us: piece_products(): pl.pallas_call(functools.partial(product_kernel, dims, tiles, orders), na...]
    ppermute x62 -> x44, starting transfers between devices: 43.4 us -> 31.8 us  [swap(): return lax.ppermute(value, axis, [(i, i ^ offset) for i in range(size)])]
    convert_element_type x17 -> x13, other arithmetic: 13.7 us -> 23 us  [the longest x6 12.4 us: advance(): keeps.append((keep[cut:].astype(f32) + got[cut:].astype(f32)).astype(bf16))]
    concatenate x11 -> x4, other arithmetic: 9.59 us -> 0.28 us  [advance_spread(): jnp.concatenate(p, axis=0)]
    transpose x0 -> x2, local copies, waits for them, and re-layouts: none -> 8.15 us  [the longest x1 4.69 us: local(): jnp.transpose(normed)]
  transfers between devices with their start and end apart: 70 -> 52, of which waited for: 21 -> 21; matrix products, arithmetic and copies ran while one was open for 20% -> 28% of each run, Pallas kernels for 21% -> 23%
where the time goes in v2:
time: 586 us; the launch traced here: 577 us
  Pallas kernels  173 us (30%)
  waiting for transfers between devices  163 us (28%)
  matrix products  76.8 us (13%)
  other arithmetic  56.7 us (10%)
  starting transfers between devices  48.9 us (8%)
  local copies, waits for them, and re-layouts  42.4 us (7%)
  between operations  15.8 us (3%)
    ppermute x44, waiting for transfers between devices, swap(): return lax.ppermute(value, axis, [(i, i ^ offset) for i in range(size)])  101 us
    pallas_call x6, Pallas kernels, piece_products(): pl.pallas_call(functools.partial(product_kernel, dims, tiles, orders), na...  53.9 us
    all_gather x1, waiting for transfers between devices, local(): lax.all_gather(hidden_in.astype(bf16), 'tensor', axis=1, tiled=True)  50.4 us
    pallas_call x1, Pallas kernels, attention_backward(): pl.pallas_call(functools.partial(backward_kernel, seq.shape[1], slots, lo...  43.6 us
    pallas_call x3, Pallas kernels, spread(): pl.pallas_call(functools.partial(spread_kernel, quarter, layout), name='s...  42.9 us
    pallas_call x1, Pallas kernels, attention_forward(): pl.pallas_call(functools.partial(forward_kernel, seq.shape[1], slots, loc...  33.1 us
    ppermute x44, starting transfers between devices, swap(): return lax.ppermute(value, axis, [(i, i ^ offset) for i in range(size)])  31.8 us
    unnamed x111, local copies, waits for them, and re-layouts  18.2 us
  transfers between devices with their start and end apart: 52, of which 21 were waited for; matrix products, arithmetic and copies ran while one was open for 28% of the time, Pallas kernels for 23%

profile of v2, /device:TPU:0, one launch (start us, length us, event | category | flops | bytes accessed | tf_op | source)
XLA Modules:
  0.0 577.1 jit_solution(16384911865305323003)
XLA Ops:
  16.6 8.8 %copy.65 = bf16[2048,3,512]{0,2,1:T(8,128)(2,1)} copy(bf16[2048,3,512]{2,0,1:T(8,128)(2,1)} %param.27) | data formatting | bytes 12582912 | tf_op args[3]
  26.0 50.4 %all-gather.3.cloned.1.call-done = bf16[768,2048]{1,0:T(8,128)(2,1)} async-done(((bf16[768,512]{1,0:T(8,128)(2,1)}), bf16[768,2048]{1,0:T(8,128)(2,1)}) %all-gather.3.cloned.1.call-update) | async-done | bytes 3145744 | tf_op jit(solution)/shard_map/all_gather | solution.py:629
  78.9 2.8 fusion.2
  81.8 9.5 %broadcast_add_fusion = f32[768,3,512]{0,2,1:T(8,128)S(1)} fusion(f32[3,512]{1,0:T(4,128)S(1)} %copy-done.41, bf16[2048,3,512]{2,0,1:T(8,128)(2,1)} %param.27, f32[2048]{0:T(1024)S(1)} %copy-done.30, f32[2048]{0:T(1024)S(1)} %copy-done.27, f32[768]{0:T(1024)S(1)} %add_rsqrt_fusion, f32[768]{0:T(1024)S(1)} %broadcast_multiply_fusion, ...), kind=kOutput, calls=%fused_computation.48 | convolution fusion | flops 4842455040 | bytes 14184448 | tf_op jit(solution)/shard_map/td,dcf->cft/dot_general | solution.py:642
  93.7 2.9 fusion.41
  96.5 4.7 copy.70.refs_0_.refs_1_.refs_2_.refs_3_
  104.8 4.6 all-to-all-start
  109.4 12.6 %fusion.17 = (bf16[768,2048]{1,0:T(8,128)(2,1)}, f32[768,2048]{1,0:T(8,128)S(1)}) fusion(f32[2048]{0:T(1024)S(1)} %copy-done.42, bf16[2048,2048]{1,0:T(8,128)(2,1)} %param.31, f32[2048]{0:T(1024)S(1)} %copy-done.30, f32[2048]{0:T(1024)S(1)} %copy-done.27, f32[768]{0:T(1024)S(1)} %add_rsqrt_fusion, f32[768]{0:T(1024)S(1)} %broadcast_multiply_fusion, ...), kind=kOutput, calls=%fused_computation.23 | convolution fusion | flops 6467616768 | bytes 21002240 | tf_op jit(solution)/shard_map/dot_general | solution.py:656
  122.0 2.7 copy-done.4
  124.7 3.1 fusion.25
  127.8 4.7 copy.69.refs_0_.refs_1_.refs_2_.refs_3_
  132.5 8.1 %all-gather.5.cloned.1.call-done.refs_4_.refs_5_.refs_6_.refs_7_.refs_8_ = bf16[768,2048]{1,0:T(8,128)(2,1)} async-done(((bf16[768,512]{1,0:T(8,128)(2,1)}), bf16[768,2048]{1,0:T(8,128)(2,1)}) %all-gather.5.cloned.1.call-update) | async-done | bytes 3145744 | tf_op jit(solution)/shard_map/all_gather | solution.py:630
  140.6 8.1 %piece_products.6 = bf16[1024,2048]{1,0:T(8,128)(2,1)} custom-call(s32[4]{0:T(128)S(1)} %broadcast_xor_fusion.1.table_ref, bf16[2048,768]{1,0:T(8,128)(2,1)} %copy.69.refs_0_.refs_1_.refs_2_.refs_3_, bf16[2048,768]{1,0:T(8,128)(2,1)} %copy.69.refs_0_.refs_1_.refs_2_.refs_3_, bf16[2048,768]{1,0:T(8,128)(2,1)} %copy.69.refs_0_.refs_1_.refs_2_.refs_3_, ...), custom_call_target="tpu_custom_call" | custom-call | flops 3221225472 | bytes 11534336 | tf_op jit(solution)/shard_map/piece_products/pallas_call | solution.py:404
  148.8 2.7 fusion.37
  151.5 4.7 collective-permute-done.refs_5_
  156.2 8.9 %piece_products.7 = (bf16[512,1024]{1,0:T(8,128)(2,1)S(1)}, bf16[512,1024]{1,0:T(8,128)(2,1)}, bf16[512,1024]{1,0:T(8,128)(2,1)}, bf16[512,1024]{1,0:T(8,128)(2,1)}) custom-call(s32[4]{0:T(128)S(1)} %broadcast_xor_fusion.2.table_ref, bf16[2048,768]{1,0:T(8,128)(2,1)} %copy.69.refs_0_.refs_1_.refs_2_.refs_3_, ...), custom_call_target="tpu_custom_call" | custom-call | flops 3221225472 | bytes 11534336 | tf_op jit(solution)/shard_map/piece_products/pallas_call | solution.py:404
  168.0 13.9 %fusion.9.refs_4_ = bf16[768,2048]{1,0:T(8,128)(2,1)} fusion(f32[768,2048]{1,0:T(8,128)S(1)} %bitcast.85, bf16[768,2048]{1,0:T(8,128)(2,1)S(1)} %copy-done.1, bf16[2048,2048]{1,0:T(8,128)(2,1)} %param.33), kind=kOutput, calls=%fused_computation.15 | convolution fusion | flops 6473908224 | bytes 20971520 | tf_op jit(solution)/shard_map/td,fd->tf/dot_general | solution.py:677
  182.0 8.3 %collective-permute-done.1 = bf16[512,1024]{1,0:T(8,128)(2,1)S(1)} collective-permute-done((bf16[512,1024]{1,0:T(8,128)(2,1)S(1)}, bf16[512,1024]{1,0:T(8,128)(2,1)S(1)}, u32[]{:S(2)}, u32[]{:S(2)}) %collective-permute-start.1) | collective-permute-done | bytes 1048608 | tf_op jit(solution)/shard_map/ppermute | solution.py:299
  191.8 7.8 %piece_products.8 = bf16[1024,2048]{1,0:T(8,128)(2,1)} custom-call(s32[4]{0:T(128)S(1)} %broadcast_xor_fusion.1.table_ref, bf16[2048,768]{1,0:T(8,128)(2,1)} %copy.70.refs_0_.refs_1_.refs_2_.refs_3_, bf16[2048,768]{1,0:T(8,128)(2,1)} %copy.70.refs_0_.refs_1_.refs_2_.refs_3_, bf16[2048,768]{1,0:T(8,128)(2,1)} %copy.70.refs_0_.refs_1_.refs_2_.refs_3_, ...), custom_call_target="tpu_custom_call" | custom-call | flops 3221225472 | bytes 11534336 | tf_op jit(solution)/shard_map/piece_products/pallas_call | solution.py:404
  202.0 4.2 all-to-all-start.1
  206.2 2.7 add_convert_fusion.18
  213.7 8.8 %piece_products.9 = (bf16[512,1024]{1,0:T(8,128)(2,1)S(1)}, bf16[512,1024]{1,0:T(8,128)(2,1)}, bf16[512,1024]{1,0:T(8,128)(2,1)}, bf16[512,1024]{1,0:T(8,128)(2,1)}) custom-call(s32[4]{0:T(128)S(1)} %broadcast_xor_fusion.2.table_ref, bf16[2048,768]{1,0:T(8,128)(2,1)} %copy.70.refs_0_.refs_1_.refs_2_.refs_3_, ...), custom_call_target="tpu_custom_call" | custom-call | flops 3221225472 | bytes 11534336 | tf_op jit(solution)/shard_map/piece_products/pallas_call | solution.py:404
  223.2 33.1 %attention_forward.1 = (bf16[8,64,768]{2,1,0:T(8,128)(2,1)}, f32[8,6656]{1,0:T(8,128)}, bf16[64,6656]{1,0:T(8,128)(2,1)}) custom-call(s32[96]{0:T(128)} %pad_add_fusion.1.place_ref, s32[2,3]{1,0:T(2,128)} %pad_add_fusion.seq_ref, s32[1]{0:T(128)} %bitcast.19.rank_ref, bf16[8,192,768]{2,1,0:T(8,128)(2,1)} %all-to-all-done.refs_0_), custom_call_target="tpu_custom_call" | custom-call | flops 19327352832 | bytes 4718592 | tf_op jit(solution)/shard_map/attention_forward/pallas_call | solution.py:239
  263.5 3.0 add_convert_fusion.11
  269.0 3.7 all-to-all-start.2
  276.2 43.6 %attention_backward.1 = bf16[8,192,768]{2,1,0:T(8,128)(2,1)} custom-call(s32[96]{0:T(128)} %pad_add_fusion.1.place_ref, s32[2,3]{1,0:T(2,128)} %pad_add_fusion.seq_ref, s32[1]{0:T(128)} %bitcast.19.rank_ref, bf16[8,192,768]{2,1,0:T(8,128)(2,1)} %all-to-all-done.refs_0_, bf16[8,64,768]{2,1,0:T(8,128)(2,1)} %all-to-all-done.1.refs_1_, ...), custom_call_target="tpu_custom_call" | custom-call | flops 48318382080 | bytes 9437184 | tf_op jit(solution)/shard_map/attention_backward/pallas_call | solution.py:270
  319.9 4.4 all-to-all-start.3
  324.3 10.2 %fusion.46 = f32[768,2048]{1,0:T(8,128)S(1)} fusion(bf16[768,2048]{1,0:T(8,128)(2,1)} %get-tuple-element.186, bf16[2048,2048]{1,0:T(8,128)(2,1)} %param.33), kind=kOutput, calls=%fused_computation.138 | convolution fusion | flops 6442450944 | bytes 17825792 | tf_op jit(solution)/shard_map/dot_general | solution.py:704
  334.5 3.7 add_convert_fusion
  338.3 12.0 %fusion.47 = f32[768,2048]{1,0:T(8,128)} fusion(bf16[768,2048]{1,0:T(8,128)(2,1)} %fusion.9.refs_4_, bf16[2048,2048]{1,0:T(8,128)(2,1)} %param.31), kind=kOutput, calls=%fused_computation.139 | convolution fusion | flops 6442450944 | bytes 17825792 | tf_op jit(solution)/shard_map/tf,df->td/dot_general | solution.py:709
  350.2 3.5 all-to-all-done.3
  353.7 3.5 copy.72
  357.2 8.5 %piece_products.10 = bf16[1024,2048]{1,0:T(8,128)(2,1)} custom-call(s32[4]{0:T(128)S(1)} %broadcast_xor_fusion.1.table_ref, bf16[2048,768]{1,0:T(8,128)(2,1)} %copy.70.refs_0_.refs_1_.refs_2_.refs_3_, bf16[2048,768]{1,0:T(8,128)(2,1)} %copy.70.refs_0_.refs_1_.refs_2_.refs_3_, bf16[2048,768]{1,0:T(8,128)(2,1)} %copy.70.refs_0_.refs_1_.refs_2_.refs_3_, ...), custom_call_target="tpu_custom_call" | custom-call | flops 3221225472 | bytes 11534336 | tf_op jit(solution)/shard_map/piece_products/pallas_call | solution.py:404
  370.9 12.2 %multiply_reduce_fusion.1 = (f32[768]{0:T(1024)S(1)}, f32[768]{0:T(1024)S(1)}, bf16[768,2048]{1,0:T(8,128)(2,1)}, f32[768,2048]{1,0:T(8,128)}) fusion(f32[2048]{0:T(1024)S(1)} %copy-done.28, f32[768]{0:T(1024)S(1)} %copy-done.24, f32[768]{0:T(1024)S(1)} %copy-done.26, bf16[768,2048]{1,0:T(8,128)(2,1)S(1)} %copy-done.3, f32[768,2048]{1,0:T(8,128)S(1)} %bitcast.88, ...), kind=kOutput, calls=%fused_computation.37 | convolution fusion | flops 4845991936 | bytes 27545600 | tf_op jit(solution)/shard_map/hcet,ched->td/dot_general | solution.py:732
  383.1 11.3 %collective-permute-done.14.refs_5_ = bf16[512,1024]{1,0:T(8,128)(2,1)S(1)} collective-permute-done((bf16[512,1024]{1,0:T(8,128)(2,1)}, bf16[512,1024]{1,0:T(8,128)(2,1)S(1)}, u32[]{:S(2)}, u32[]{:S(2)}) %collective-permute-start.14) | collective-permute-done | bytes 1048608 | tf_op jit(solution)/shard_map/ppermute | solution.py:299
  400.8 9.5 %collective-permute-done.15 = bf16[256,1024]{1,0:T(8,128)(2,1)S(1)} collective-permute-done((bf16[256,1024]{1,0:T(8,128)(2,1)S(1)}, bf16[256,1024]{1,0:T(8,128)(2,1)S(1)}, u32[]{:S(2)}, u32[]{:S(2)}) %collective-permute-start.15) | collective-permute-done | bytes 524320 | tf_op jit(solution)/shard_map/ppermute | solution.py:299
  410.3 11.8 %piece_products.11 = (bf16[512,1024]{1,0:T(8,128)(2,1)S(1)}, bf16[512,1024]{1,0:T(8,128)(2,1)}, bf16[512,1024]{1,0:T(8,128)(2,1)}, bf16[512,1024]{1,0:T(8,128)(2,1)}) custom-call(s32[4]{0:T(128)S(1)} %broadcast_xor_fusion.2.table_ref, bf16[2048,768]{1,0:T(8,128)(2,1)} %copy.70.refs_0_.refs_1_.refs_2_.refs_3_, ...), custom_call_target="tpu_custom_call" | custom-call | flops 3221225472 | bytes 11534336 | tf_op jit(solution)/shard_map/piece_products/pallas_call | solution.py:404
  427.5 14.2 %spread.3 = f32[2048,2048]{1,0:T(8,128)} custom-call(s32[16]{0:T(128)S(1)} %broadcast_xor_fusion.table_ref, bf16[512,1024]{1,0:T(8,128)(2,1)S(1)} %constant_dynamic-update-slice_fusion.refs_0_, bf16[512,1024]{1,0:T(8,128)(2,1)} %collective-permute-done.13.refs_1_, bf16[512,1024]{1,0:T(8,128)(2,1)S(1)} %collective-permute-done.17.refs_2_, ...), custom_call_target="tpu_custom_call" | custom-call | bytes 25165824 | tf_op jit(solution)/shard_map/spread/pallas_call | solution.py:569
  441.7 6.7 %collective-permute-done.22.refs_5_ = bf16[512,1024]{1,0:T(8,128)(2,1)} collective-permute-done((bf16[512,1024]{1,0:T(8,128)(2,1)S(1)}, bf16[512,1024]{1,0:T(8,128)(2,1)}, u32[]{:S(2)}, u32[]{:S(2)}) %collective-permute-start.22) | collective-permute-done | bytes 1048608 | tf_op jit(solution)/shard_map/ppermute | solution.py:299
  450.0 21.7 %collective-permute-done.23 = bf16[512,1024]{1,0:T(8,128)(2,1)S(1)} collective-permute-done((bf16[512,1024]{1,0:T(8,128)(2,1)S(1)}, bf16[512,1024]{1,0:T(8,128)(2,1)S(1)}, u32[]{:S(2)}, u32[]{:S(2)}) %collective-permute-start.23) | collective-permute-done | bytes 1048608 | tf_op jit(solution)/shard_map/ppermute | solution.py:299
  477.8 3.9 multiply_reduce_fusion.2
  483.2 14.3 %spread.4 = f32[2048,2048]{1,0:T(8,128)} custom-call(s32[16]{0:T(128)S(1)} %broadcast_xor_fusion.table_ref, bf16[512,1024]{1,0:T(8,128)(2,1)S(1)} %pad_maximum_fusion.1.refs_0_, bf16[512,1024]{1,0:T(8,128)(2,1)} %collective-permute-done.21.refs_1_, bf16[512,1024]{1,0:T(8,128)(2,1)S(1)} %collective-permute-done.27.refs_2_, ...), custom_call_target="tpu_custom_call" | custom-call | bytes 25165824 | tf_op jit(solution)/shard_map/spread/pallas_call | solution.py:569
  503.1 9.0 %collective-permute-done.34 = bf16[256,1024]{1,0:T(8,128)(2,1)S(1)} collective-permute-done((bf16[256,1024]{1,0:T(8,128)(2,1)S(1)}, bf16[256,1024]{1,0:T(8,128)(2,1)S(1)}, u32[]{:S(2)}, u32[]{:S(2)}) %collective-permute-start.34) | collective-permute-done | bytes 524320 | tf_op jit(solution)/shard_map/ppermute | solution.py:299
  512.1 2.6 collective-permute-done.33
  525.5 12.9 %collective-permute-done.38.refs_5_ = bf16[512,1024]{1,0:T(8,128)(2,1)} collective-permute-done((bf16[512,1024]{1,0:T(8,128)(2,1)S(1)}, bf16[512,1024]{1,0:T(8,128)(2,1)}, u32[]{:S(2)}, u32[]{:S(2)}) %collective-permute-start.38) | collective-permute-done | bytes 1048608 | tf_op jit(solution)/shard_map/ppermute | solution.py:299
  539.9 3.9 convert_reduce_fusion.3
  545.4 3.5 collective-permute-done.42
  555.2 14.4 %spread.5 = (f32[3,2048,512]{2,1,0:T(8,128)}, f32[512,2048]{1,0:T(8,128)}) custom-call(s32[16]{0:T(128)S(1)} %broadcast_xor_fusion.table_ref, bf16[512,1024]{1,0:T(8,128)(2,1)S(1)} %pad_maximum_fusion.3.refs_0_, bf16[512,1024]{1,0:T(8,128)(2,1)S(1)} %collective-permute-done.37.refs_1_, bf16[512,1024]{1,0:T(8,128)(2,1)} %collective-permute-done.35.refs_2_, ...), custom_call_target="tpu_custom_call" | custom-call | bytes 25165824 | tf_op jit(solution)/shard_map/spread/pallas_call | solution.py:569
  (277 shorter events, 95.5 us)
Async XLA Ops:
  7.2 69.1 %all-gather.3.cloned.1.call-start = ((), (), s32[]{:S(2)}) async-start(), calls=%async_computation.6 | async-start | bytes 3932160 | tf_op jit(solution)/shard_map/all_gather | solution.py:629
  9.7 130.9 %all-gather.5.cloned.1.call-start = ((), (), s32[]{:S(2)}) async-start(), calls=%async_computation.7 | async-start | bytes 3932160 | tf_op jit(solution)/shard_map/all_gather | solution.py:630
  104.8 35.9 %all-to-all-start = ((bf16[8,192,768]{2,1,0:T(8,128)(2,1)}), bf16[8,192,768]{2,1,0:T(8,128)(2,1)}, u32[]{:S(2)}, u32[]{:S(2)}) async-start(bf16[8,192,768]{2,1,0:T(8,128)(2,1)} %pad_maximum_fusion), calls=%async_computation | async-start | bytes 4718592 | tf_op jit(solution)/shard_map/all_to_all | solution.py:620
  148.7 7.5 %collective-permute-start = (bf16[1024,2048]{1,0:T(8,128)(2,1)}, bf16[1024,2048]{1,0:T(8,128)(2,1)}, u32[]{:S(2)}, u32[]{:S(2)}) collective-permute-start(bf16[1024,2048]{1,0:T(8,128)(2,1)} %piece_products.6), channel_id=1, source_target_pairs={{0,4},{4,0},{8,12},{12,8},{16,20},{20,16},{24,28},{28,24},{1,5},{5... | collective-permute-start | bytes 12582920 | tf_op jit(solution)/shard_map/ppermute | solution.py:299
  165.1 25.2 %collective-permute-start.1 = (bf16[512,1024]{1,0:T(8,128)(2,1)S(1)}, bf16[512,1024]{1,0:T(8,128)(2,1)S(1)}, u32[]{:S(2)}, u32[]{:S(2)}) collective-permute-start(bf16[512,1024]{1,0:T(8,128)(2,1)S(1)} %get-tuple-element.145), channel_id=1, source_target_pairs={{0,8},{4,12},{8,0},{12,4},{16,24},{20,28},{24,16},{28,20},{1,9},{5... | collective-permute-start | bytes 3145736 | tf_op jit(solution)/shard_map/ppermute | solution.py:299
  166.6 25.2 %collective-permute-start.2 = (bf16[512,1024]{1,0:T(8,128)(2,1)}, bf16[512,1024]{1,0:T(8,128)(2,1)}, u32[]{:S(2)}, u32[]{:S(2)}) collective-permute-start(bf16[512,1024]{1,0:T(8,128)(2,1)} %get-tuple-element.146), channel_id=1, source_target_pairs={{0,16},{4,20},{8,24},{12,28},{16,0},{20,4},{24,8},{28,12},{1,17},{... | collective-permute-start | bytes 3145736 | tf_op jit(solution)/shard_map/ppermute | solution.py:299
  199.6 14.1 %collective-permute-start.3 = (bf16[1024,2048]{1,0:T(8,128)(2,1)}, bf16[1024,2048]{1,0:T(8,128)(2,1)}, u32[]{:S(2)}, u32[]{:S(2)}) collective-permute-start(bf16[1024,2048]{1,0:T(8,128)(2,1)} %piece_products.8), channel_id=1, source_target_pairs={{0,4},{4,0},{8,12},{12,8},{16,20},{20,16},{24,28},{28,24},{1,5},{5... | collective-permute-start | bytes 12582920 | tf_op jit(solution)/shard_map/ppermute | solution.py:299
  202.0 54.3 %all-to-all-start.1 = ((bf16[8,64,768]{2,1,0:T(8,128)(2,1)}), bf16[8,64,768]{2,1,0:T(8,128)(2,1)}, u32[]{:S(2)}, u32[]{:S(2)}) async-start(bf16[8,64,768]{2,1,0:T(8,128)(2,1)} %bitcast.20), calls=%async_computation.1 | async-start | bytes 1572864 | tf_op jit(solution)/shard_map/all_to_all | solution.py:620
  208.9 47.4 %collective-permute-start.5 = (bf16[256,1024]{1,0:T(8,128)(2,1)}, bf16[256,1024]{1,0:T(8,128)(2,1)}, u32[]{:S(2)}, u32[]{:S(2)}) collective-permute-start(bf16[256,1024]{1,0:T(8,128)(2,1)} %get-tuple-element.275), channel_id=1, source_target_pairs={{0,8},{4,12},{8,0},{12,4},{16,24},{20,28},{24,16},{28,20},{1,9},{5... | collective-permute-start | bytes 1572872 | tf_op jit(solution)/shard_map/ppermute | solution.py:299
  212.2 44.1 %collective-permute-start.4 = (bf16[256,1024]{1,0:T(8,128)(2,1)}, bf16[256,1024]{1,0:T(8,128)(2,1)}, u32[]{:S(2)}, u32[]{:S(2)}) collective-permute-start(bf16[256,1024]{1,0:T(8,128)(2,1)} %get-tuple-element.277), channel_id=1, source_target_pairs={{0,16},{4,20},{8,24},{12,28},{16,0},{20,4},{24,8},{28,12},{1,17},{... | collective-permute-start | bytes 1572872 | tf_op jit(solution)/shard_map/ppermute | solution.py:299
  222.5 33.8 %collective-permute-start.6 = (bf16[512,1024]{1,0:T(8,128)(2,1)S(1)}, bf16[512,1024]{1,0:T(8,128)(2,1)S(1)}, u32[]{:S(2)}, u32[]{:S(2)}) collective-permute-start(bf16[512,1024]{1,0:T(8,128)(2,1)S(1)} %get-tuple-element.162), channel_id=1, source_target_pairs={{0,8},{4,12},{8,0},{12,4},{16,24},{20,28},{24,16},{28,20},{1,9},{5... | collective-permute-start | bytes 3145736 | tf_op jit(solution)/shard_map/ppermute | solution.py:299
  223.0 33.3 %collective-permute-start.7 = (bf16[512,1024]{1,0:T(8,128)(2,1)}, bf16[512,1024]{1,0:T(8,128)(2,1)}, u32[]{:S(2)}, u32[]{:S(2)}) collective-permute-start(bf16[512,1024]{1,0:T(8,128)(2,1)} %get-tuple-element.163), channel_id=1, source_target_pairs={{0,16},{4,20},{8,24},{12,28},{16,0},{20,4},{24,8},{28,12},{1,17},{... | collective-permute-start | bytes 3145736 | tf_op jit(solution)/shard_map/ppermute | solution.py:299
  258.5 61.3 %collective-permute-start.9 = (bf16[256,1024]{1,0:T(8,128)(2,1)S(1)}, bf16[256,1024]{1,0:T(8,128)(2,1)}, u32[]{:S(2)}, u32[]{:S(2)}) collective-permute-start(bf16[256,1024]{1,0:T(8,128)(2,1)S(1)} %add_convert_fusion.14), channel_id=1, source_target_pairs={{0,8},{4,12},{8,0},{12,4},{16,24},{20,28},{24,16},{28,20},{1,9},{5... | collective-permute-start | bytes 1572872 | tf_op jit(solution)/shard_map/ppermute | solution.py:299
  261.9 57.9 %collective-permute-start.8 = (bf16[256,1024]{1,0:T(8,128)(2,1)S(1)}, bf16[256,1024]{1,0:T(8,128)(2,1)}, u32[]{:S(2)}, u32[]{:S(2)}) collective-permute-start(bf16[256,1024]{1,0:T(8,128)(2,1)S(1)} %add_convert_fusion.15), channel_id=1, source_target_pairs={{0,16},{4,20},{8,24},{12,28},{16,0},{20,4},{24,8},{28,12},{1,17},{... | collective-permute-start | bytes 1572872 | tf_op jit(solution)/shard_map/ppermute | solution.py:299
  269.0 50.9 %all-to-all-start.2 = ((bf16[8,64,768]{2,1,0:T(8,128)(2,1)}), bf16[8,64,768]{2,1,0:T(8,128)(2,1)S(1)}, u32[]{:S(2)}, u32[]{:S(2)}) async-start(bf16[8,64,768]{2,1,0:T(8,128)(2,1)} %get-tuple-element.183), calls=%async_computation.2 | async-start | bytes 1572864 | tf_op jit(solution)/shard_map/all_to_all | solution.py:623
  272.7 47.1 %collective-permute-start.11 = (bf16[256,1024]{1,0:T(8,128)(2,1)}, bf16[256,1024]{1,0:T(8,128)(2,1)}, u32[]{:S(2)}, u32[]{:S(2)}) collective-permute-start(bf16[256,1024]{1,0:T(8,128)(2,1)} %get-tuple-element.271), channel_id=1, source_target_pairs={{0,8},{4,12},{8,0},{12,4},{16,24},{20,28},{24,16},{28,20},{1,9},{5... | collective-permute-start | bytes 1572872 | tf_op jit(solution)/shard_map/ppermute | solution.py:299
  274.7 45.1 %collective-permute-start.10 = (bf16[256,1024]{1,0:T(8,128)(2,1)}, bf16[256,1024]{1,0:T(8,128)(2,1)}, u32[]{:S(2)}, u32[]{:S(2)}) collective-permute-start(bf16[256,1024]{1,0:T(8,128)(2,1)} %get-tuple-element.273), channel_id=1, source_target_pairs={{0,16},{4,20},{8,24},{12,28},{16,0},{20,4},{24,8},{28,12},{1,17},{... | collective-permute-start | bytes 1572872 | tf_op jit(solution)/shard_map/ppermute | solution.py:299
  319.9 33.8 %all-to-all-start.3 = ((bf16[8,192,768]{2,1,0:T(8,128)(2,1)}), bf16[8,192,768]{2,1,0:T(8,128)(2,1)}, u32[]{:S(2)}, u32[]{:S(2)}) async-start(bf16[8,192,768]{2,1,0:T(8,128)(2,1)} %attention_backward.1), calls=%async_computation.4 | async-start | bytes 4718592 | tf_op jit(solution)/shard_map/all_to_all | solution.py:623
  324.2 153.6 %reduce-scatter.3.cloned.1.call-start = ((), (), s32[]{:S(2)}) async-start(), calls=%async_computation.8 | async-start | bytes 3932160 | tf_op jit(solution)/shard_map/reduce_scatter | solution.py:706
  338.2 201.7 %reduce-scatter.5.cloned.1.call-start = ((), (), s32[]{:S(2)}) async-start(), calls=%async_computation.9 | async-start | bytes 3932160 | tf_op jit(solution)/shard_map/reduce_scatter | solution.py:741
  365.7 29.9 %collective-permute-start.12 = (bf16[1024,2048]{1,0:T(8,128)(2,1)}, bf16[1024,2048]{1,0:T(8,128)(2,1)}, u32[]{:S(2)}, u32[]{:S(2)}) collective-permute-start(bf16[1024,2048]{1,0:T(8,128)(2,1)} %piece_products.10), channel_id=1, source_target_pairs={{0,4},{4,0},{8,12},{12,8},{16,20},{20,16},{24,28},{28,24},{1,5},{5... | collective-permute-start | bytes 12582920 | tf_op jit(solution)/shard_map/ppermute | solution.py:299
  368.6 25.8 %collective-permute-start.14 = (bf16[512,1024]{1,0:T(8,128)(2,1)}, bf16[512,1024]{1,0:T(8,128)(2,1)S(1)}, u32[]{:S(2)}, u32[]{:S(2)}) collective-permute-start(bf16[512,1024]{1,0:T(8,128)(2,1)} %constant_dynamic-update-slice_fusion.2.refs_4_), channel_id=1, source_target_pairs={{0,16},{4,20},{8,24},{12,28},{16,0},{20,4},{24,8},{28,12},{1,17},{... | collective-permute-start | bytes 3145736 | tf_op jit(solution)/shard_map/ppermute | solution.py:299
  370.2 25.4 %collective-permute-start.13 = (bf16[512,1024]{1,0:T(8,128)(2,1)S(1)}, bf16[512,1024]{1,0:T(8,128)(2,1)}, u32[]{:S(2)}, u32[]{:S(2)}) collective-permute-start(bf16[512,1024]{1,0:T(8,128)(2,1)S(1)} %constant_dynamic-update-slice_fusion.refs_0_), channel_id=1, source_target_pairs={{0,8},{4,12},{8,0},{12,4},{16,24},{20,28},{24,16},{28,20},{1,9},{5... | collective-permute-start | bytes 3145736 | tf_op jit(solution)/shard_map/ppermute | solution.py:299
  396.9 13.4 %collective-permute-start.15 = (bf16[256,1024]{1,0:T(8,128)(2,1)S(1)}, bf16[256,1024]{1,0:T(8,128)(2,1)S(1)}, u32[]{:S(2)}, u32[]{:S(2)}) collective-permute-start(bf16[256,1024]{1,0:T(8,128)(2,1)S(1)} %add_convert_fusion.9), channel_id=1, source_target_pairs={{0,16},{4,20},{8,24},{12,28},{16,0},{20,4},{24,8},{28,12},{1,17},{... | collective-permute-start | bytes 1572872 | tf_op jit(solution)/shard_map/ppermute | solution.py:299
  398.5 25.2 %collective-permute-start.18 = (bf16[512,1024]{1,0:T(8,128)(2,1)}, bf16[512,1024]{1,0:T(8,128)(2,1)S(1)}, u32[]{:S(2)}, u32[]{:S(2)}) collective-permute-start(bf16[512,1024]{1,0:T(8,128)(2,1)} %constant_dynamic-update-slice_fusion.2.refs_4_), channel_id=1, source_target_pairs={{0,4},{4,0},{8,12},{12,8},{16,20},{20,16},{24,28},{28,24},{1,5},{5... | collective-permute-start | bytes 3145736 | tf_op jit(solution)/shard_map/ppermute | solution.py:299
  398.5 25.6 %collective-permute-start.17 = (bf16[512,1024]{1,0:T(8,128)(2,1)S(1)}, bf16[512,1024]{1,0:T(8,128)(2,1)S(1)}, u32[]{:S(2)}, u32[]{:S(2)}) collective-permute-start(bf16[512,1024]{1,0:T(8,128)(2,1)S(1)} %constant_dynamic-update-slice_fusion.refs_0_), channel_id=1, source_target_pairs={{0,4},{4,0},{8,12},{12,8},{16,20},{20,16},{24,28},{28,24},{1,5},{5... | collective-permute-start | bytes 3145736 | tf_op jit(solution)/shard_map/ppermute | solution.py:299
  399.0 26.8 %collective-permute-start.19 = (bf16[512,1024]{1,0:T(8,128)(2,1)}, bf16[512,1024]{1,0:T(8,128)(2,1)S(1)}, u32[]{:S(2)}, u32[]{:S(2)}) collective-permute-start(bf16[512,1024]{1,0:T(8,128)(2,1)} %collective-permute-done.13.refs_1_), channel_id=1, source_target_pairs={{0,4},{4,0},{8,12},{12,8},{16,20},{20,16},{24,28},{28,24},{1,5},{5... | collective-permute-start | bytes 3145736 | tf_op jit(solution)/shard_map/ppermute | solution.py:299
  400.3 21.8 %collective-permute-start.16 = (bf16[256,1024]{1,0:T(8,128)(2,1)S(1)}, bf16[256,1024]{1,0:T(8,128)(2,1)S(1)}, u32[]{:S(2)}, u32[]{:S(2)}) collective-permute-start(bf16[256,1024]{1,0:T(8,128)(2,1)S(1)} %add_convert_fusion.8), channel_id=1, source_target_pairs={{0,8},{4,12},{8,0},{12,4},{16,24},{20,28},{24,16},{28,20},{1,9},{5... | collective-permute-start | bytes 1572872 | tf_op jit(solution)/shard_map/ppermute | solution.py:299
  410.3 16.2 %collective-permute-start.20 = (bf16[512,1024]{1,0:T(8,128)(2,1)}, bf16[512,1024]{1,0:T(8,128)(2,1)S(1)}, u32[]{:S(2)}, u32[]{:S(2)}) collective-permute-start(bf16[512,1024]{1,0:T(8,128)(2,1)} %copy-done.14), channel_id=1, source_target_pairs={{0,4},{4,0},{8,12},{12,8},{16,20},{20,16},{24,28},{28,24},{1,5},{5... | collective-permute-start | bytes 3145736 | tf_op jit(solution)/shard_map/ppermute | solution.py:299
  422.2 26.2 %collective-permute-start.22 = (bf16[512,1024]{1,0:T(8,128)(2,1)S(1)}, bf16[512,1024]{1,0:T(8,128)(2,1)}, u32[]{:S(2)}, u32[]{:S(2)}) collective-permute-start(bf16[512,1024]{1,0:T(8,128)(2,1)S(1)} %pad_maximum_fusion.2.refs_4_), channel_id=1, source_target_pairs={{0,16},{4,20},{8,24},{12,28},{16,0},{20,4},{24,8},{28,12},{1,17},{... | collective-permute-start | bytes 3145736 | tf_op jit(solution)/shard_map/ppermute | solution.py:299
  423.8 26.2 %collective-permute-start.21 = (bf16[512,1024]{1,0:T(8,128)(2,1)S(1)}, bf16[512,1024]{1,0:T(8,128)(2,1)}, u32[]{:S(2)}, u32[]{:S(2)}) collective-permute-start(bf16[512,1024]{1,0:T(8,128)(2,1)S(1)} %pad_maximum_fusion.1.refs_0_), channel_id=1, source_target_pairs={{0,8},{4,12},{8,0},{12,4},{16,24},{20,28},{24,16},{28,20},{1,9},{5... | collective-permute-start | bytes 3145736 | tf_op jit(solution)/shard_map/ppermute | solution.py:299
  424.2 47.5 %collective-permute-start.23 = (bf16[512,1024]{1,0:T(8,128)(2,1)S(1)}, bf16[512,1024]{1,0:T(8,128)(2,1)S(1)}, u32[]{:S(2)}, u32[]{:S(2)}) collective-permute-start(bf16[512,1024]{1,0:T(8,128)(2,1)S(1)} %get-tuple-element.216), channel_id=1, source_target_pairs={{0,8},{4,12},{8,0},{12,4},{16,24},{20,28},{24,16},{28,20},{1,9},{5... | collective-permute-start | bytes 3145736 | tf_op jit(solution)/shard_map/ppermute | solution.py:299
  425.9 45.8 %collective-permute-start.24 = (bf16[512,1024]{1,0:T(8,128)(2,1)}, bf16[512,1024]{1,0:T(8,128)(2,1)S(1)}, u32[]{:S(2)}, u32[]{:S(2)}) collective-permute-start(bf16[512,1024]{1,0:T(8,128)(2,1)} %get-tuple-element.217), channel_id=1, source_target_pairs={{0,16},{4,20},{8,24},{12,28},{16,0},{20,4},{24,8},{28,12},{1,17},{... | collective-permute-start | bytes 3145736 | tf_op jit(solution)/shard_map/ppermute | solution.py:299
  426.5 48.8 %collective-permute-start.28 = (bf16[512,1024]{1,0:T(8,128)(2,1)S(1)}, bf16[512,1024]{1,0:T(8,128)(2,1)S(1)}, u32[]{:S(2)}, u32[]{:S(2)}) collective-permute-start(bf16[512,1024]{1,0:T(8,128)(2,1)S(1)} %pad_maximum_fusion.2.refs_4_), channel_id=1, source_target_pairs={{0,4},{4,0},{8,12},{12,8},{16,20},{20,16},{24,28},{28,24},{1,5},{5... | collective-permute-start | bytes 3145736 | tf_op jit(solution)/shard_map/ppermute | solution.py:299
  448.4 34.8 %collective-permute-start.27 = (bf16[512,1024]{1,0:T(8,128)(2,1)S(1)}, bf16[512,1024]{1,0:T(8,128)(2,1)S(1)}, u32[]{:S(2)}, u32[]{:S(2)}) collective-permute-start(bf16[512,1024]{1,0:T(8,128)(2,1)S(1)} %pad_maximum_fusion.1.refs_0_), channel_id=1, source_target_pairs={{0,4},{4,0},{8,12},{12,8},{16,20},{20,16},{24,28},{28,24},{1,5},{5... | collective-permute-start | bytes 3145736 | tf_op jit(solution)/shard_map/ppermute | solution.py:299
  471.7 11.5 %collective-permute-start.29 = (bf16[512,1024]{1,0:T(8,128)(2,1)}, bf16[512,1024]{1,0:T(8,128)(2,1)}, u32[]{:S(2)}, u32[]{:S(2)}) collective-permute-start(bf16[512,1024]{1,0:T(8,128)(2,1)} %collective-permute-done.21.refs_1_), channel_id=1, source_target_pairs={{0,4},{4,0},{8,12},{12,8},{16,20},{20,16},{24,28},{28,24},{1,5},{5... | collective-permute-start | bytes 3145736 | tf_op jit(solution)/shard_map/ppermute | solution.py:299
  471.7 11.5 %collective-permute-start.30 = (bf16[512,1024]{1,0:T(8,128)(2,1)}, bf16[512,1024]{1,0:T(8,128)(2,1)}, u32[]{:S(2)}, u32[]{:S(2)}) collective-permute-start(bf16[512,1024]{1,0:T(8,128)(2,1)} %collective-permute-done.22.refs_5_), channel_id=1, source_target_pairs={{0,4},{4,0},{8,12},{12,8},{16,20},{20,16},{24,28},{28,24},{1,5},{5... | collective-permute-start | bytes 3145736 | tf_op jit(solution)/shard_map/ppermute | solution.py:299
  473.6 23.9 %collective-permute-start.26 = (bf16[256,1024]{1,0:T(8,128)(2,1)}, bf16[256,1024]{1,0:T(8,128)(2,1)}, u32[]{:S(2)}, u32[]{:S(2)}) collective-permute-start(bf16[256,1024]{1,0:T(8,128)(2,1)} %get-tuple-element.267), channel_id=1, source_target_pairs={{0,8},{4,12},{8,0},{12,4},{16,24},{20,28},{24,16},{28,20},{1,9},{5... | collective-permute-start | bytes 1572872 | tf_op jit(solution)/shard_map/ppermute | solution.py:299
  476.2 21.3 %collective-permute-start.25 = (bf16[256,1024]{1,0:T(8,128)(2,1)}, bf16[256,1024]{1,0:T(8,128)(2,1)}, u32[]{:S(2)}, u32[]{:S(2)}) collective-permute-start(bf16[256,1024]{1,0:T(8,128)(2,1)} %get-tuple-element.269), channel_id=1, source_target_pairs={{0,16},{4,20},{8,24},{12,28},{16,0},{20,4},{24,8},{28,12},{1,17},{... | collective-permute-start | bytes 1572872 | tf_op jit(solution)/shard_map/ppermute | solution.py:299
  498.8 13.3 %collective-permute-start.34 = (bf16[256,1024]{1,0:T(8,128)(2,1)S(1)}, bf16[256,1024]{1,0:T(8,128)(2,1)S(1)}, u32[]{:S(2)}, u32[]{:S(2)}) collective-permute-start(bf16[256,1024]{1,0:T(8,128)(2,1)S(1)} %add_convert_fusion.2), channel_id=1, source_target_pairs={{0,8},{4,12},{8,0},{12,4},{16,24},{20,28},{24,16},{28,20},{1,9},{5... | collective-permute-start | bytes 1572872 | tf_op jit(solution)/shard_map/ppermute | solution.py:299
  501.6 13.1 %collective-permute-start.33 = (bf16[256,1024]{1,0:T(8,128)(2,1)S(1)}, bf16[256,1024]{1,0:T(8,128)(2,1)S(1)}, u32[]{:S(2)}, u32[]{:S(2)}) collective-permute-start(bf16[256,1024]{1,0:T(8,128)(2,1)S(1)} %add_convert_fusion.3), channel_id=1, source_target_pairs={{0,16},{4,20},{8,24},{12,28},{16,0},{20,4},{24,8},{28,12},{1,17},{... | collective-permute-start | bytes 1572872 | tf_op jit(solution)/shard_map/ppermute | solution.py:299
  514.8 23.5 %collective-permute-start.38 = (bf16[512,1024]{1,0:T(8,128)(2,1)S(1)}, bf16[512,1024]{1,0:T(8,128)(2,1)}, u32[]{:S(2)}, u32[]{:S(2)}) collective-permute-start(bf16[512,1024]{1,0:T(8,128)(2,1)S(1)} %pad_maximum_fusion.4.refs_4_), channel_id=1, source_target_pairs={{0,16},{4,20},{8,24},{12,28},{16,0},{20,4},{24,8},{28,12},{1,17},{... | collective-permute-start | bytes 3145736 | tf_op jit(solution)/shard_map/ppermute | solution.py:299
  516.3 23.1 %collective-permute-start.37 = (bf16[512,1024]{1,0:T(8,128)(2,1)S(1)}, bf16[512,1024]{1,0:T(8,128)(2,1)S(1)}, u32[]{:S(2)}, u32[]{:S(2)}) collective-permute-start(bf16[512,1024]{1,0:T(8,128)(2,1)S(1)} %pad_maximum_fusion.3.refs_0_), channel_id=1, source_target_pairs={{0,8},{4,12},{8,0},{12,4},{16,24},{20,28},{24,16},{28,20},{1,9},{5... | collective-permute-start | bytes 3145736 | tf_op jit(solution)/shard_map/ppermute | solution.py:299
  520.4 4.5 collective-permute-start.32
  524.9 26.0 %collective-permute-start.36 = (bf16[512,1024]{1,0:T(8,128)(2,1)S(1)}, bf16[512,1024]{1,0:T(8,128)(2,1)}, u32[]{:S(2)}, u32[]{:S(2)}) collective-permute-start(bf16[512,1024]{1,0:T(8,128)(2,1)S(1)} %pad_maximum_fusion.4.refs_4_), channel_id=1, source_target_pairs={{0,4},{4,0},{8,12},{12,8},{16,20},{20,16},{24,28},{28,24},{1,5},{5... | collective-permute-start | bytes 3145736 | tf_op jit(solution)/shard_map/ppermute | solution.py:299
  525.0 25.9 %collective-permute-start.35 = (bf16[512,1024]{1,0:T(8,128)(2,1)S(1)}, bf16[512,1024]{1,0:T(8,128)(2,1)}, u32[]{:S(2)}, u32[]{:S(2)}) collective-permute-start(bf16[512,1024]{1,0:T(8,128)(2,1)S(1)} %pad_maximum_fusion.3.refs_0_), channel_id=1, source_target_pairs={{0,4},{4,0},{8,12},{12,8},{16,20},{20,16},{24,28},{28,24},{1,5},{5... | collective-permute-start | bytes 3145736 | tf_op jit(solution)/shard_map/ppermute | solution.py:299
  539.4 11.5 %collective-permute-start.39 = (bf16[512,1024]{1,0:T(8,128)(2,1)S(1)}, bf16[512,1024]{1,0:T(8,128)(2,1)}, u32[]{:S(2)}, u32[]{:S(2)}) collective-permute-start(bf16[512,1024]{1,0:T(8,128)(2,1)S(1)} %collective-permute-done.37.refs_1_), channel_id=1, source_target_pairs={{0,4},{4,0},{8,12},{12,8},{16,20},{20,16},{24,28},{28,24},{1,5},{5... | collective-permute-start | bytes 3145736 | tf_op jit(solution)/shard_map/ppermute | solution.py:299
  539.4 11.5 %collective-permute-start.40 = (bf16[512,1024]{1,0:T(8,128)(2,1)}, bf16[512,1024]{1,0:T(8,128)(2,1)}, u32[]{:S(2)}, u32[]{:S(2)}) collective-permute-start(bf16[512,1024]{1,0:T(8,128)(2,1)} %collective-permute-done.38.refs_5_), channel_id=1, source_target_pairs={{0,4},{4,0},{8,12},{12,8},{16,20},{20,16},{24,28},{28,24},{1,5},{5... | collective-permute-start | bytes 3145736 | tf_op jit(solution)/shard_map/ppermute | solution.py:299
  (55 other events, 979.1 us)
Sparse Core Ops, SparseCore 0:
  10.2 66.1 all-gather.2
  78.5 62.0 all-gather.4
  338.3 59.4 reduce-scatter.2
  400.0 60.2 reduce-scatter.4
